TPU v7x, 256 devices: a whole 4x4x8 slice. The times are simulated.
256 devices in a mesh: band: 16 (over z_lo, y, core), section: 16 (over z_hi, x).
Axes of the slice: x: 4, y: 4, z: 8 (z_hi: 4, z_lo: 2; z = z_hi * 2 + z_lo), core: 2. Of those that a mesh axis runs over, the one named last changes fastest.
Arguments:
- fields: bfloat16 [4, 64, 128, 256], P(None, 'band'), may hold values from -6 to 6
- cotangent: bfloat16 [4, 64, 128, 256], P(None, 'band'), may hold values from -6 to 6
- kernels: bfloat16 [16, 3, 3, 256, 256], P('section'), may hold values from -0.0625 to 0.0625
- biases: float32 [16, 256], P('section'), may hold values from -2 to 2
Outputs:
- block_states: bfloat16 [16, 4, 64, 128, 256], P('section', None, 'band')
- field_grads: bfloat16 [16, 4, 64, 128, 256], P('section', None, 'band')
All inputs are finite; a program needn't handle non-finite values.
Results may differ from a plain program's by a relative error of at most 0.023.
Values may be sent and summed in bfloat16 or wider, within the bound.
No kernel may reach another device: no remote copies, remote signals or barrier semaphores. Data moves between devices by JAX's collectives and lax.ppermute only.
A program may use at most 64 MiB of HBM per device.

v0:
```python
import jax
import jax.numpy as jnp
from jax import lax
from jax.experimental import pallas as pl
from jax.experimental.pallas import tpu as pltpu
from jax.sharding import PartitionSpec as P


DEPTH = 4
CHUNKS = (1, 2)
EXTRA = 16
SLOPE_BASE = (0, 10, 18, 24)
SLOPE_ROWS = 28
VMEM_LIMIT = 52 * 1024 * 1024
BF16 = jnp.bfloat16
F32 = jnp.float32


def spread_columns(ref, base, value, shift, across, channels):
    count = value.shape[0]
    cells = value.reshape(count // across, across, channels)
    before = pltpu.roll(cells, shift % across, 1).reshape(count, channels)
    after = pltpu.roll(cells, -shift % across, 1).reshape(count, channels)
    ref[pl.ds(base, count), 0:channels] = before.astype(BF16)
    ref[pl.ds(base, count), channels : 2 * channels] = value.astype(BF16)
    ref[pl.ds(base, count), 2 * channels : 3 * channels] = after.astype(BF16)


def copy_weights(flags, mine, theirs, weights, bias, sems, bias_sems):
    parity, turn, place = flags[2], flags[3], flags[4]
    rows = weights.shape[1] // (2 * DEPTH)
    slot = flags[5]
    behind = (0, 1, 3, 2)
    for side, pieces in enumerate((mine, theirs)):
        core = parity if side == 0 else 1 - parity
        for outer in range(DEPTH):
            for inner in range(DEPTH):
                source = pieces[outer] if outer < 3 else pieces[3 + inner // 2]
                index = inner if outer < 3 else inner % 2
                first, second = behind[inner], behind[outer]
                layer = (place - jnp.where(core == 0, first, second) + DEPTH) % DEPTH
                part = (turn - jnp.where(core == 0, second, first) + DEPTH) % DEPTH
                at = core * DEPTH + part
                pltpu.make_async_copy(
                    source.at[index, slot, pl.ds(0, rows)],
                    weights.at[layer, pl.ds(pl.multiple_of(at * rows, 32), rows)],
                    sems.at[layer, at],
                ).start()
                if side == 0 and bias is not None:
                    pltpu.make_async_copy(
                        source.at[index, slot, pl.ds(rows, EXTRA)], bias.at[layer, part], bias_sems.at[layer, part]
                    ).start()

    def wait(layer):
        for at in range(2 * DEPTH):
            pltpu.make_async_copy(
                mine[0].at[0, 0, pl.ds(0, rows)], weights.at[layer, pl.ds(at * rows, rows)], sems.at[layer, at]
            ).wait()
        if bias is not None:
            for part in range(DEPTH):
                pltpu.make_async_copy(
                    mine[0].at[0, 0, pl.ds(rows, EXTRA)], bias.at[layer, part], bias_sems.at[layer, part]
                ).wait()

    return wait


def forward_kernel(flags, own, outside, inside, *refs):
    mine, theirs = refs[:5], refs[5:10]
    edge, all_slopes, kept_states, all_outside, all_inside = refs[14:19]
    slopes, states, wide, other, weights, bias, sems, bias_sems, out_sems = refs[19:]
    block, group = flags[6], flags[7]
    save = pltpu.make_async_copy(slopes, all_slopes.at[block], out_sems.at[0])
    keep = pltpu.make_async_copy(states, kept_states, out_sems.at[1])
    rows, across, channels = states.shape[1:]
    wait = copy_weights(flags, mine, theirs, weights, bias, sems, bias_sems)
    last_block = (block + DEPTH - 1) % DEPTH
    pass_on = [
        pltpu.make_async_copy(piece.at[pl.ds(rows, rows + 2)], kept.at[last_block], out_sems.at[2 + index])
        for index, (piece, kept) in enumerate(((outside, all_outside), (inside, all_inside)))
    ]
    for copy in pass_on:
        copy.start()
    odd = flags[2] == 1
    for part in range(3):

        @pl.loop(0, rows)
        def _(row, part=part):
            base = pl.multiple_of((part * rows + row) * across, across)
            if part == 1:
                line = own[row].astype(F32)
            else:
                pair = (inside, outside) if part == 0 else (outside, inside)
                line = jnp.where(odd, pair[0][row].astype(F32), pair[1][row].astype(F32))
            spread_columns(wide, base, line, 1, across, channels)

    def poles(ref):
        middle = across // 2
        top, bottom = rows * across, (2 * rows - 1) * across

        @pl.when(flags[0] == 1)
        def _():
            ref[top - across : top - middle, :] = ref[top + middle : top + across, :]
            ref[top - middle : top, :] = ref[top : top + middle, :]

        @pl.when(flags[1] == 1)
        def _():
            ref[bottom + across : bottom + across + middle, :] = ref[bottom + middle : bottom + across, :]
            ref[bottom + across + middle : bottom + 2 * across, :] = ref[bottom : bottom + middle, :]

    for layer in range(DEPTH):
        source, target = (wide, other) if layer % 2 == 0 else (other, wide)
        poles(source)
        wait(layer)
        reach = DEPTH - 1 - layer
        parts = bias[layer, 0].astype(F32)
        offset = (parts[0:1] + parts[1:2]) + parts[2:3]

        height = rows + 2 * reach
        for index in range(0, height, CHUNKS[0]):
            count = min(CHUNKS[0], height - index)
            step = count * across
            base = (rows - reach + index) * across
            preact = None
            for tap in range(3):
                term = jnp.dot(
                    source[pl.ds(base + (tap - 1) * across, step), :],
                    weights[layer, tap * 3 * channels : (tap + 1) * 3 * channels, :],
                    preferred_element_type=F32,
                )
                preact = term if preact is None else preact + term
            preact = preact + offset
            sigmoid = 0.5 * jnp.tanh(0.5 * preact) + 0.5
            silu = preact * sigmoid
            slope = (sigmoid + silu * (1.0 - sigmoid)).astype(BF16).reshape(count, across, channels)
            before = source[pl.ds(base, step), channels : 2 * channels].astype(F32)
            result = (before + silu).astype(BF16)
            if layer < DEPTH - 1:
                spread_columns(target, base, result.astype(F32), 1, across, channels)
            slopes[pl.ds(SLOPE_BASE[layer] + index, count)] = slope
            if layer == DEPTH - 1:
                edge[pl.ds(index, count)] = result.reshape(count, across, channels)

        if layer < DEPTH - 1:
            own_cells = target[rows * across : 2 * rows * across, channels : 2 * channels]
            states[layer] = own_cells.reshape(rows, across, channels)
    states[DEPTH - 1] = edge[0:rows]
    edge[rows : 2 * rows] = slopes[SLOPE_BASE[3] : SLOPE_BASE[3] + rows]
    edge[2 * rows :] = slopes[SLOPE_BASE[2] + 2 : SLOPE_BASE[2] + 4]
    save.start()

    @pl.when(block == group)
    def _():
        keep.start()
        keep.wait()

    for copy in [save] + pass_on:
        copy.wait()


def backward_kernel(flags, own, outside, inside, all_slopes, all_outside, all_inside, last_outside, last_inside, *refs):
    mine, theirs = refs[:5], refs[5:10]
    rows = own.shape[0]
    current, kept_grads = refs[11:13]
    grads, slopes, far_above, far_below, upstream, wide, added, weights, sems, out_sems = refs[13:]
    block, group = flags[6], flags[7]
    odd = flags[2] == 1
    for swapped in range(2):

        @pl.when((flags[2] == swapped) & (block < DEPTH - 1))
        def _(swapped=swapped):
            ends = (all_inside, all_outside) if swapped else (all_outside, all_inside)
            for index, (source, target) in enumerate(zip(ends, (far_above, far_below))):
                pltpu.make_async_copy(source.at[block], target, out_sems.at[index]).start()

        @pl.when((flags[2] == swapped) & (block == DEPTH - 1))
        def _(swapped=swapped):
            ends = (last_inside, last_outside) if swapped else (last_outside, last_inside)
            for index, (source, target) in enumerate(zip(ends, (far_above, far_below))):
                pltpu.make_async_copy(source.at[pl.ds(rows, rows + 2)], target, out_sems.at[index]).start()

    pltpu.make_async_copy(all_slopes.at[block], slopes, out_sems.at[2]).start()
    loads = [
        pltpu.make_async_copy(source.at[block], target, out_sems.at[index])
        for index, (source, target) in enumerate(
            ((all_outside, far_above), (all_inside, far_below), (all_slopes, slopes))
        )
    ]
    keep = pltpu.make_async_copy(grads, kept_grads, out_sems.at[3])
    rows, across, channels = own.shape
    middle = across // 2
    wait = copy_weights(flags, mine, theirs, weights, None, sems, None)
    for row in range(rows):
        lines = outside[row], inside[row]
        for part, line in enumerate((jnp.where(odd, lines[1], lines[0]), own[row], jnp.where(odd, lines[0], lines[1]))):
            at = (part * rows + row) * across
            upstream[at : at + across] = line
    added[...] = jnp.zeros(added.shape, F32)
    for load in loads:
        load.wait()
    contract = (((1,), (1,)), ((), ()))

    def tap_weight(layer, tap, column):
        at = (tap * 3 + column) * channels
        return weights[layer, at : at + channels, :]

    for layer in reversed(range(DEPTH)):

        def deltas(first, count, slope_ref, slope_base):
            @pl.loop(0, count)
            def _(index):
                base = pl.multiple_of((first + index) * across, across)
                delta = upstream[pl.ds(base, across)].astype(F32) * slope_ref[slope_base + index].astype(F32)
                spread_columns(wide, base, delta.astype(BF16).astype(F32), -1, across, channels)

        if layer == 3:
            deltas(0, rows, far_above, 0)
            deltas(rows, rows, slopes, SLOPE_BASE[3])
            deltas(2 * rows, rows, far_below, 0)
        elif layer == 2:
            deltas(1, 2, far_above, rows)
            deltas(rows - 1, rows + 2, slopes, SLOPE_BASE[2])
            deltas(2 * rows + 1, 2, far_below, rows)
        else:
            deltas(rows - 1 - layer, rows + 2 + 2 * layer, slopes, SLOPE_BASE[layer] + (2 if layer == 0 else 0))
        top, bottom = rows * across, (2 * rows - 1) * across
        wait(layer)

        def edge_terms(base, tap, layer=layer):
            for piece in range(2):
                start = base + (1 - piece) * middle
                total = None
                for column in range(3):
                    term = lax.dot_general(
                        wide[start : start + middle, column * channels : (column + 1) * channels],
                        tap_weight(layer, tap, column), contract, preferred_element_type=F32,
                    )
                    total = term if total is None else total + term
                added[base + piece * middle : base + (piece + 1) * middle, :] = total

        @pl.when(flags[0] == 1)
        def _():
            wide[top - across : top, :] = jnp.zeros((across, 3 * channels), BF16)
            edge_terms(top, 0)

        @pl.when(flags[1] == 1)
        def _():
            wide[bottom + across : bottom + 2 * across, :] = jnp.zeros((across, 3 * channels), BF16)
            edge_terms(bottom, 2)

        height = rows + 2 * layer
        for index in range(0, height, CHUNKS[1]):
            count = min(CHUNKS[1], height - index)
            step = count * across
            base = (rows - layer + index) * across
            total = upstream[pl.ds(base, step)].astype(F32) + added[pl.ds(base, step)]
            for tap in range(3):
                for column in range(3):
                    total = total + lax.dot_general(
                        wide[pl.ds(base + (1 - tap) * across, step), column * channels : (column + 1) * channels],
                        tap_weight(layer, tap, column), contract, preferred_element_type=F32,
                    )
            upstream[pl.ds(base, step)] = total.astype(BF16)

        grads[layer] = upstream[rows * across : 2 * rows * across].reshape(rows, across, channels)
    current[...] = grads[0]

    @pl.when(block == group)
    def _():
        keep.start()
        keep.wait()


def shift(block, axis, pairs):
    return lax.ppermute(block, axis, pairs)


def on_device(fields, cotangent, kernels, biases):
    band_count = lax.axis_size("band")
    section_count = lax.axis_size("section")
    micro_count, rows, across, channels = fields.shape
    groups = section_count // DEPTH
    band = lax.axis_index("band")
    section = lax.axis_index("section")
    group = section // DEPTH
    place = section % DEPTH
    parity = band % 2
    turn = band // 2 % DEPTH
    bias = biases[0]
    high = lax.reduce_precision(bias, 8, 7)
    middle = lax.reduce_precision(bias - high, 8, 7)
    low = bias - high - middle
    extra = jnp.stack([high, middle, low] + [jnp.zeros_like(bias)] * (EXTRA - 3)).astype(BF16)

    def route(move):
        pairs = []
        for b in range(band_count):
            for s in range(section_count):
                low, y, core, z, x = b // (2 * DEPTH), b // 2 % DEPTH, b % 2, s // DEPTH, s % DEPTH
                y, core, z, x = move(y, core, z, x)
                to = (low * 2 * DEPTH + y % DEPTH * 2 + core) * section_count + z % DEPTH * DEPTH + x % DEPTH
                pairs.append((b * section_count + s, to))
        return pairs

    def carry(block, pairs):
        return lax.ppermute(block, ("band", "section"), pairs)

    def around(block, forth, back):
        middle = block.shape[0] // 2
        behind, ahead = carry(block, route(forth)), carry(block, route(back))
        return behind, ahead, carry(behind[:middle], route(forth)), carry(ahead[middle:], route(back))

    def joined(block, forth, back):
        behind, ahead, low, high = around(block, forth, back)
        return jnp.stack([block, behind, ahead, jnp.concatenate([low, high])])

    outside = [pair for i in range(1, band_count - 1, 2) for pair in ((i, i + 1), (i + 1, i))]

    partner = [(i, i ^ 1) for i in range(band_count)]

    def edges(block):
        return shift(block, "band", outside), shift(block, "band", partner)

    current, upstream = (lax.dynamic_index_in_dim(block, place, 0, keepdims=False) for block in (fields, cotangent))
    edge = jnp.concatenate([current, upstream, upstream[:2]])

    quarter = 9 * channels // 2 // DEPTH
    start = (parity * DEPTH + turn) * quarter
    piece = lax.dynamic_slice_in_dim(kernels.reshape(9 * channels, channels), start, quarter, 0)
    piece = jnp.concatenate([piece, extra])
    hbm = pl.BlockSpec(memory_space=pl.ANY)

    def after(block, *others):
        return pl.pallas_call(
            lambda *refs: None,
            out_shape=jax.ShapeDtypeStruct(block.shape, BF16),
            in_specs=[hbm] * (1 + len(others)),
            out_specs=hbm,
            input_output_aliases={0: 0},
            name="after",
        )(block, *others)

    forth, back = route(lambda y, c, z, x: (y, c, z + 1, x)), route(lambda y, c, z, x: (y, c, z - 1, x))
    behind, ahead = carry(piece, forth), carry(piece, back)
    low, high = carry(behind[: (quarter + EXTRA) // 2], forth), carry(ahead[(quarter + EXTRA) // 2 :], back)
    edge = after(edge, behind)
    edge_outside, edge_inside = edges(edge)

    def take_edges(piece, outside, inside, out, first, second, sems):
        copies = [
            pltpu.make_async_copy(source.at[pl.ds(rows, rows)], target, sems.at[index])
            for index, (source, target) in enumerate(((outside, first), (inside, second)))
        ]
        for copy in copies:
            copy.start()
        for copy in copies:
            copy.wait()

    piece = jnp.stack([piece, behind, ahead, jnp.concatenate([low, high])])
    part_shape = jax.ShapeDtypeStruct((rows, across, channels), BF16)
    piece, start_outside, start_inside = pl.pallas_call(
        take_edges,
        out_shape=(jax.ShapeDtypeStruct(piece.shape, BF16), part_shape, part_shape),
        in_specs=[hbm] * 3,
        out_specs=(hbm,) * 3,
        input_output_aliases={0: 0},
        scratch_shapes=[pltpu.SemaphoreType.DMA((2,))],
        name="take_edges",
    )(piece, edge_outside, edge_inside)
    piece = joined(
        piece,
        lambda y, c, z, x: (y + c, c, z, x + 1 - c),
        lambda y, c, z, x: (y - c, c, z, x - 1 + c),
    )
    ring = around(
        piece,
        lambda y, c, z, x: (y + 1 - c, c, z, x + c),
        lambda y, c, z, x: (y - 1 + c, c, z, x - c),
    )
    mine = (piece,) + ring
    theirs = tuple(carry(block, route(lambda y, c, z, x: (y, 1 - c, z, x))) for block in mine)

    row_shape = (rows, across, channels)
    smem = pl.BlockSpec(memory_space=pltpu.SMEM)
    vmem = pl.BlockSpec(memory_space=pltpu.VMEM)
    hbm = pl.BlockSpec(memory_space=pl.ANY)
    wide = pltpu.VMEM((3 * rows * across, 3 * channels), BF16)
    weight_room = pltpu.VMEM((DEPTH, 9 * channels, channels), BF16)
    bias_room = pltpu.VMEM((DEPTH, DEPTH, EXTRA, channels), BF16)
    sems = pltpu.SemaphoreType.DMA((DEPTH, 2 * DEPTH))
    bias_sems = pltpu.SemaphoreType.DMA((DEPTH, DEPTH))
    params = pltpu.CompilerParams(vmem_limit_bytes=VMEM_LIMIT)

    def shaped(*shape):
        return jax.ShapeDtypeStruct(shape, BF16)

    cells = (across, channels)

    def flags_of(block):
        slot = (group - block) % groups
        slot = jnp.where(slot == 2, 3, jnp.where(slot == 3, 2, slot))
        return jnp.stack(
            [band == 0, band == band_count - 1, parity, turn, place, slot, block, group]
        ).astype(jnp.int32)

    forward = pl.pallas_call(
        forward_kernel,
        out_shape=(
            shaped(2 * rows + 2, *cells),
            shaped(groups, SLOPE_ROWS, *cells),
            shaped(DEPTH, *row_shape),
            shaped(groups, rows + 2, *cells),
            shaped(groups, rows + 2, *cells),
        ),
        in_specs=[smem, vmem, vmem, vmem] + [hbm] * 14,
        out_specs=(vmem,) + (hbm,) * 4,
        input_output_aliases={14: 1, 15: 2, 16: 3, 17: 4},
        scratch_shapes=[
            pltpu.VMEM((SLOPE_ROWS, *cells), BF16),
            pltpu.VMEM((DEPTH, *row_shape), BF16),
            wide,
            wide,
            weight_room,
            bias_room,
            sems,
            bias_sems,
            pltpu.SemaphoreType.DMA((4,)),
        ],
        compiler_params=params,
        name="forward",
    )
    backward = pl.pallas_call(
        backward_kernel,
        out_shape=(shaped(*row_shape), shaped(DEPTH, *row_shape)),
        in_specs=[smem] + [vmem] * 3 + [hbm] * 16,
        out_specs=(vmem, hbm),
        input_output_aliases={19: 1},
        scratch_shapes=[
            pltpu.VMEM((DEPTH, *row_shape), BF16),
            pltpu.VMEM((SLOPE_ROWS, *cells), BF16),
            pltpu.VMEM((rows + 2, *cells), BF16),
            pltpu.VMEM((rows + 2, *cells), BF16),
            pltpu.VMEM((3 * rows * across, channels), BF16),
            wide,
            pltpu.VMEM((3 * rows * across, channels), F32),
            weight_room,
            sems,
            pltpu.SemaphoreType.DMA((4,)),
        ],
        compiler_params=params,
        name="backward",
    )

    def forward_step(block, state):
        edge, outside, inside, *kept = state
        edge, *kept = forward(flags_of(block), edge, outside, inside, *mine, *theirs, *kept)
        return edge, *edges(edge), *kept

    room = pl.pallas_call(
        lambda *refs: None,
        out_shape=(
            shaped(groups, SLOPE_ROWS, *cells),
            shaped(DEPTH, *row_shape),
            shaped(groups, rows + 2, *cells),
            shaped(groups, rows + 2, *cells),
            shaped(DEPTH, *row_shape),
        ),
        out_specs=(hbm,) * 5,
        name="room",
    )()
    state = (edge, edge_outside, edge_inside, *room[:4])
    edge, last_outside, last_inside, slopes, states, far_outside, far_inside = lax.fori_loop(
        0, groups, forward_step, state
    )

    def deliver(kept):
        out = jnp.zeros((micro_count,) + row_shape, BF16)
        out = lax.dynamic_update_index_in_dim(out, lax.dynamic_index_in_dim(kept, place, 0, keepdims=False), place, 0)
        for step in range(1, DEPTH):
            send = lax.dynamic_index_in_dim(kept, (place + step) % DEPTH, 0, keepdims=False)
            pairs = [(g * DEPTH + p, g * DEPTH + (p + step) % DEPTH) for g in range(groups) for p in range(DEPTH)]
            received = shift(send, "section", pairs)
            out = lax.dynamic_update_index_in_dim(out, received, (place - step) % DEPTH, 0)
        return out[None]

    delivered = deliver(states)

    def backward_step(step, state):
        upstream, above, below, grads = state
        block = groups - 1 - step
        upstream, grads = backward(
            flags_of(block), upstream, above, below, slopes, far_outside, far_inside, last_outside, last_inside,
            *mine, *theirs, grads,
        )
        above, below = lax.cond(block > 0, edges, lambda _: (above, below), upstream)
        return upstream, above, below, grads

    state = (upstream, start_outside, start_inside, room[4])
    grads = lax.fori_loop(0, groups, backward_step, state)[3]

    return delivered, deliver(grads)


def solution(mesh):
    placed = (
        P(None, "band", None, None),
        P(None, "band", None, None),
        P("section", None, None, None, None),
        P("section", None),
    )
    return jax.shard_map(
        on_device,
        mesh=mesh,
        in_specs=placed,
        out_specs=(P("section", None, "band", None, None), P("section", None, "band", None, None)),
        check_vma=False,
    )
```

profile of v0, /device:TPU:25, one launch (start us, length us, event | category | flops | bytes accessed | tf_op | source)
XLA Modules:
  0.0 357.2 jit_solution(17971104279572313539)
XLA Ops:
  2.1 3.1 collective-permute-start.4
  7.3 5.2 %collective-permute-done.4.refs_1_ = bf16[304,256]{1,0:T(8,128)(2,1)S(1)} collective-permute-done((bf16[304,256]{1,0:T(8,128)(2,1)S(1)}, bf16[304,256]{1,0:T(8,128)(2,1)S(1)}, u32[]{:S(2)}, u32[]{:S(2)}) %collective-permute-start.4) | collective-permute-done | bytes 155680 | tf_op jit(solution)/shard_map/ppermute | solution.py:306
  13.2 6.2 %collective-permute-start.5 = (bf16[10,128,256]{2,1,0:T(8,128)(2,1)S(1)}, bf16[10,128,256]{2,1,0:T(8,128)(2,1)}, u32[]{:S(2)}, u32[]{:S(2)}) collective-permute-start(bf16[10,128,256]{2,1,0:T(8,128)(2,1)S(1)} %after.1), channel_id=1, source_target_pairs={{16,32},{32,16},{48,64},{64,48},{80,96},{96,80},{112,128},{128,112... | collective-permute-start | bytes 1966088 | tf_op jit(solution)/shard_map/ppermute | solution.py:275
  22.8 6.8 %collective-permute-done.7 = bf16[304,256]{1,0:T(8,128)(2,1)S(1)} collective-permute-done((bf16[304,256]{1,0:T(8,128)(2,1)S(1)}, bf16[304,256]{1,0:T(8,128)(2,1)S(1)}, u32[]{:S(2)}, u32[]{:S(2)}) %collective-permute-start.7) | collective-permute-done | bytes 155680 | tf_op jit(solution)/shard_map/ppermute | solution.py:306
  29.6 3.2 collective-permute-start.9
  36.1 17.0 %take_edges.1 = (bf16[4,304,256]{2,1,0:T(8,128)(2,1)}, bf16[4,128,256]{2,1,0:T(8,128)(2,1)}, bf16[4,128,256]{2,1,0:T(8,128)(2,1)}) custom-call(bf16[4,304,256]{2,1,0:T(8,128)(2,1)} %pad_maximum_fusion.2.piece, bf16[10,128,256]{2,1,0:T(8,128)(2,1)} %collective-permute-done.5.outside, ...), custom_call_target="tpu_custom_call", output_to_operand_aliasing={{0}: (0, {})} | custom-call | tf_op jit(solution)/shard_map/take_edges/pallas_call | solution.py:361
  55.2 8.0 %collective-permute-done.10 = bf16[4,304,256]{2,1,0:T(8,128)(2,1)S(1)} collective-permute-done((bf16[4,304,256]{2,1,0:T(8,128)(2,1)}, bf16[4,304,256]{2,1,0:T(8,128)(2,1)S(1)}, u32[]{:S(2)}, u32[]{:S(2)}) %collective-permute-start.10) | collective-permute-done | bytes 622624 | tf_op jit(solution)/shard_map/ppermute | solution.py:306
  64.9 4.1 %collective-permute-done.12 = bf16[2,304,256]{2,1,0:T(8,128)(2,1)S(1)} collective-permute-done((bf16[2,304,256]{2,1,0:T(8,128)(2,1)S(1)}, bf16[2,304,256]{2,1,0:T(8,128)(2,1)S(1)}, u32[]{:S(2)}, u32[]{:S(2)}) %collective-permute-start.12) | collective-permute-done | bytes 311328 | tf_op jit(solution)/shard_map/ppermute | solution.py:306
  69.0 2.6 collective-permute-done.13
  76.2 2.4 collective-permute-start.18
  78.6 25.9 %collective-permute-done.14 = bf16[4,4,304,256]{3,2,1,0:T(8,128)(2,1)} collective-permute-done((bf16[4,4,304,256]{3,2,1,0:T(8,128)(2,1)}, bf16[4,4,304,256]{3,2,1,0:T(8,128)(2,1)}, u32[]{:S(2)}, u32[]{:S(2)}) %collective-permute-start.14) | collective-permute-done | bytes 2490400 | tf_op jit(solution)/shard_map/ppermute | solution.py:306
  107.3 2.7 collective-permute-start.17
  110.1 3.3 collective-permute-start.19
  113.6 9.6 %collective-permute-done.16 = bf16[2,4,304,256]{3,2,1,0:T(8,128)(2,1)} collective-permute-done((bf16[2,4,304,256]{3,2,1,0:T(8,128)(2,1)S(1)}, bf16[2,4,304,256]{3,2,1,0:T(8,128)(2,1)}, u32[]{:S(2)}, u32[]{:S(2)}) %collective-permute-start.16) | collective-permute-done | bytes 1245216 | tf_op jit(solution)/shard_map/ppermute | solution.py:306
  123.3 2.9 collective-permute-start.21
  126.2 5.3 %collective-permute-start.22 = (bf16[2,4,304,256]{3,2,1,0:T(8,128)(2,1)}, bf16[2,4,304,256]{3,2,1,0:T(8,128)(2,1)}, u32[]{:S(2)}, u32[]{:S(2)}) collective-permute-start(bf16[2,4,304,256]{3,2,1,0:T(8,128)(2,1)} %collective-permute-done.17), channel_id=1, source_target_pairs={{0,16},{1,17},{2,18},{3,19},{4,20},{5,21},{6,22},{7,23},{8,24},{9,... | collective-permute-start | bytes 3735560 | tf_op jit(solution)/shard_map/ppermute | solution.py:306
  131.5 2.9 collective-permute-done.22
  134.4 114.4 %while.48 = (s32[]{:T(128)}, bf16[10,128,256]{2,1,0:T(8,128)(2,1)}, bf16[10,128,256]{2,1,0:T(8,128)(2,1)}, bf16[10,128,256]{2,1,0:T(8,128)(2,1)}, bf16[4,28,128,...) while((s32[]{:T(128)}, bf16[10,128,256]{2,1,0:T(8,128)(2,1)}, ...), condition=%wide.region_1.2_spmd, body=%wide.region_0.1_spmd.sunk | while | flops 20 | bytes 6554172 | solution.py:472
  134.5 12.3 %forward.8 = (bf16[10,128,256]{2,1,0:T(8,128)(2,1)S(1)}, bf16[4,28,128,256]{3,2,1,0:T(8,128)(2,1)}, bf16[4,4,128,256]{3,2,1,0:T(8,128)(2,1)}, bf16[4,6,128,256]{...) custom-call(s32[8]{0:T(128)S(1)} %stack.243.flags, ...), custom_call_target="tpu_custom_call", output_to_operand_aliasing={{1}: (14, {}), {2}: (15, {}), {3}: (16, {}), {4}: (17, {})} | custom-call | tf_op jit(solution)/shard_map/while/body/eval_jaxpr/forward/pallas_call | solution.py:456
  146.8 15.1 %collective-permute-start.2 = (bf16[10,128,256]{2,1,0:T(8,128)(2,1)S(1)}, bf16[10,128,256]{2,1,0:T(8,128)(2,1)}, u32[]{:S(2)}, u32[]{:S(2)}) collective-permute-start(bf16[10,128,256]{2,1,0:T(8,128)(2,1)S(1)} %get-tuple-element.1616), channel_id=1, source_target_pairs={{16,32},{32,16},{48,64},{64,48},{80,96},{96,80},{112,128},{128,112... | collective-permute-start | bytes 1966088 | tf_op jit(solution)/shard_map/while/body/eval_jaxpr/ppermute | solution.py:275
  162.9 7.4 %collective-permute-done.2 = bf16[10,128,256]{2,1,0:T(8,128)(2,1)} collective-permute-done((bf16[10,128,256]{2,1,0:T(8,128)(2,1)S(1)}, bf16[10,128,256]{2,1,0:T(8,128)(2,1)}, u32[]{:S(2)}, u32[]{:S(2)}) %collective-permute-start.2) | collective-permute-done | bytes 655392 | tf_op jit(solution)/shard_map/while/body/eval_jaxpr/ppermute | solution.py:275
  170.3 12.0 %forward.8 = (bf16[10,128,256]{2,1,0:T(8,128)(2,1)S(1)}, bf16[4,28,128,256]{3,2,1,0:T(8,128)(2,1)}, bf16[4,4,128,256]{3,2,1,0:T(8,128)(2,1)}, bf16[4,6,128,256]{...) custom-call(s32[8]{0:T(128)S(1)} %stack.243.flags, ...), custom_call_target="tpu_custom_call", output_to_operand_aliasing={{1}: (14, {}), {2}: (15, {}), {3}: (16, {}), {4}: (17, {})} | custom-call | tf_op jit(solution)/shard_map/while/body/eval_jaxpr/forward/pallas_call | solution.py:456
  182.3 5.5 %collective-permute-start.2 = (bf16[10,128,256]{2,1,0:T(8,128)(2,1)S(1)}, bf16[10,128,256]{2,1,0:T(8,128)(2,1)}, u32[]{:S(2)}, u32[]{:S(2)}) collective-permute-start(bf16[10,128,256]{2,1,0:T(8,128)(2,1)S(1)} %get-tuple-element.1616), channel_id=1, source_target_pairs={{16,32},{32,16},{48,64},{64,48},{80,96},{96,80},{112,128},{128,112... | collective-permute-start | bytes 1966088 | tf_op jit(solution)/shard_map/while/body/eval_jaxpr/ppermute | solution.py:275
  188.8 7.6 %collective-permute-done.2 = bf16[10,128,256]{2,1,0:T(8,128)(2,1)} collective-permute-done((bf16[10,128,256]{2,1,0:T(8,128)(2,1)S(1)}, bf16[10,128,256]{2,1,0:T(8,128)(2,1)}, u32[]{:S(2)}, u32[]{:S(2)}) %collective-permute-start.2) | collective-permute-done | bytes 655392 | tf_op jit(solution)/shard_map/while/body/eval_jaxpr/ppermute | solution.py:275
  196.5 12.0 %forward.8 = (bf16[10,128,256]{2,1,0:T(8,128)(2,1)S(1)}, bf16[4,28,128,256]{3,2,1,0:T(8,128)(2,1)}, bf16[4,4,128,256]{3,2,1,0:T(8,128)(2,1)}, bf16[4,6,128,256]{...) custom-call(s32[8]{0:T(128)S(1)} %stack.243.flags, ...), custom_call_target="tpu_custom_call", output_to_operand_aliasing={{1}: (14, {}), {2}: (15, {}), {3}: (16, {}), {4}: (17, {})} | custom-call | tf_op jit(solution)/shard_map/while/body/eval_jaxpr/forward/pallas_call | solution.py:456
  208.5 5.3 %collective-permute-start.2 = (bf16[10,128,256]{2,1,0:T(8,128)(2,1)S(1)}, bf16[10,128,256]{2,1,0:T(8,128)(2,1)}, u32[]{:S(2)}, u32[]{:S(2)}) collective-permute-start(bf16[10,128,256]{2,1,0:T(8,128)(2,1)S(1)} %get-tuple-element.1616), channel_id=1, source_target_pairs={{16,32},{32,16},{48,64},{64,48},{80,96},{96,80},{112,128},{128,112... | collective-permute-start | bytes 1966088 | tf_op jit(solution)/shard_map/while/body/eval_jaxpr/ppermute | solution.py:275
  214.8 7.8 %collective-permute-done.2 = bf16[10,128,256]{2,1,0:T(8,128)(2,1)} collective-permute-done((bf16[10,128,256]{2,1,0:T(8,128)(2,1)S(1)}, bf16[10,128,256]{2,1,0:T(8,128)(2,1)}, u32[]{:S(2)}, u32[]{:S(2)}) %collective-permute-start.2) | collective-permute-done | bytes 655392 | tf_op jit(solution)/shard_map/while/body/eval_jaxpr/ppermute | solution.py:275
  222.7 12.0 %forward.8 = (bf16[10,128,256]{2,1,0:T(8,128)(2,1)S(1)}, bf16[4,28,128,256]{3,2,1,0:T(8,128)(2,1)}, bf16[4,4,128,256]{3,2,1,0:T(8,128)(2,1)}, bf16[4,6,128,256]{...) custom-call(s32[8]{0:T(128)S(1)} %stack.243.flags, ...), custom_call_target="tpu_custom_call", output_to_operand_aliasing={{1}: (14, {}), {2}: (15, {}), {3}: (16, {}), {4}: (17, {})} | custom-call | tf_op jit(solution)/shard_map/while/body/eval_jaxpr/forward/pallas_call | solution.py:456
  234.7 5.0 %collective-permute-start.2 = (bf16[10,128,256]{2,1,0:T(8,128)(2,1)S(1)}, bf16[10,128,256]{2,1,0:T(8,128)(2,1)}, u32[]{:S(2)}, u32[]{:S(2)}) collective-permute-start(bf16[10,128,256]{2,1,0:T(8,128)(2,1)S(1)} %get-tuple-element.1616), channel_id=1, source_target_pairs={{16,32},{32,16},{48,64},{64,48},{80,96},{96,80},{112,128},{128,112... | collective-permute-start | bytes 1966088 | tf_op jit(solution)/shard_map/while/body/eval_jaxpr/ppermute | solution.py:275
  240.7 8.1 %collective-permute-done.2 = bf16[10,128,256]{2,1,0:T(8,128)(2,1)} collective-permute-done((bf16[10,128,256]{2,1,0:T(8,128)(2,1)S(1)}, bf16[10,128,256]{2,1,0:T(8,128)(2,1)}, u32[]{:S(2)}, u32[]{:S(2)}) %collective-permute-start.2) | collective-permute-done | bytes 655392 | tf_op jit(solution)/shard_map/while/body/eval_jaxpr/ppermute | solution.py:275
  248.8 79.1 %while.49 = (s32[]{:T(128)}, bf16[4,128,256]{2,1,0:T(8,128)(2,1)}, bf16[4,128,256]{2,1,0:T(8,128)(2,1)}, bf16[4,128,256]{2,1,0:T(8,128)(2,1)}, bf16[4,4,128,256]...) while((s32[]{:T(128)}, bf16[4,128,256]{2,1,0:T(8,128)(2,1)}, ...), condition=%wide.region_5.6_spmd, body=%wide.region_2.5_spmd.sunk | while | flops 23 | bytes 2622094 | solution.py:499
  248.9 11.3 %backward.8 = (bf16[4,128,256]{2,1,0:T(8,128)(2,1)S(1)}, bf16[4,4,128,256]{3,2,1,0:T(8,128)(2,1)}) custom-call(s32[8]{0:T(128)S(1)} %stack.246.flags, bf16[4,128,256]{2,1,0:T(8,128)(2,1)} %get-tuple-element.1676.own, bf16[4,128,256]{2,1,0:T(8,128)(2,1)} %get-tuple-element.1677.outside, ...), custom_call_target="tpu_custom_call", output_to_operand_aliasing={{1}: (19, {})} | custom-call | tf_op jit(solution)/shard_map/while/body/eval_jaxpr/backward/pallas_call | solution.py:491
  260.3 9.9 %conditional.2 = ((bf16[4,128,256]{2,1,0:T(8,128)(2,1)}, bf16[4,128,256]{2,1,0:T(8,128)(2,1)})) conditional(s32[]{:T(128)} %convert_element_type.44, (bf16[4,128,256]{2,1,0:T(8,128)(2,1)}, bf16[4,128,256]{2,1,0:T(8,128)(2,1)}) %tuple.93, bf16[4,128,256]{2,1,0:T(8,128)(2,1)S(1)} %get-tuple-element.1707), branch_computations={%region_3.3_spmd, %region_4.4_spmd} | conditional | bytes 2097256 | solution.py:495
  260.3 4.9 %collective-permute-start = (bf16[4,128,256]{2,1,0:T(8,128)(2,1)S(1)}, bf16[4,128,256]{2,1,0:T(8,128)(2,1)}, u32[]{:S(2)}, u32[]{:S(2)}) collective-permute-start(bf16[4,128,256]{2,1,0:T(8,128)(2,1)S(1)} %param.3), channel_id=1, source_target_pairs={{16,32},{32,16},{48,64},{64,48},{80,96},{96,80},{112,128},{128,112... | collective-permute-start | bytes 786440 | tf_op jit(solution)/shard_map/while/body/eval_jaxpr/cond/branch_1_fun/ppermute | solution.py:275
  265.3 4.9 %collective-permute-done = bf16[4,128,256]{2,1,0:T(8,128)(2,1)} collective-permute-done((bf16[4,128,256]{2,1,0:T(8,128)(2,1)S(1)}, bf16[4,128,256]{2,1,0:T(8,128)(2,1)}, u32[]{:S(2)}, u32[]{:S(2)}) %collective-permute-start) | collective-permute-done | bytes 262176 | tf_op jit(solution)/shard_map/while/body/eval_jaxpr/cond/branch_1_fun/ppermute | solution.py:275
  271.0 11.2 %backward.8 = (bf16[4,128,256]{2,1,0:T(8,128)(2,1)S(1)}, bf16[4,4,128,256]{3,2,1,0:T(8,128)(2,1)}) custom-call(s32[8]{0:T(128)S(1)} %stack.246.flags, bf16[4,128,256]{2,1,0:T(8,128)(2,1)} %get-tuple-element.1676.own, bf16[4,128,256]{2,1,0:T(8,128)(2,1)} %get-tuple-element.1677.outside, ...), custom_call_target="tpu_custom_call", output_to_operand_aliasing={{1}: (19, {})} | custom-call | tf_op jit(solution)/shard_map/while/body/eval_jaxpr/backward/pallas_call | solution.py:491
  282.2 9.9 %conditional.2 = ((bf16[4,128,256]{2,1,0:T(8,128)(2,1)}, bf16[4,128,256]{2,1,0:T(8,128)(2,1)})) conditional(s32[]{:T(128)} %convert_element_type.44, (bf16[4,128,256]{2,1,0:T(8,128)(2,1)}, bf16[4,128,256]{2,1,0:T(8,128)(2,1)}) %tuple.93, bf16[4,128,256]{2,1,0:T(8,128)(2,1)S(1)} %get-tuple-element.1707), branch_computations={%region_3.3_spmd, %region_4.4_spmd} | conditional | bytes 2097256 | solution.py:495
  282.3 5.0 %collective-permute-start = (bf16[4,128,256]{2,1,0:T(8,128)(2,1)S(1)}, bf16[4,128,256]{2,1,0:T(8,128)(2,1)}, u32[]{:S(2)}, u32[]{:S(2)}) collective-permute-start(bf16[4,128,256]{2,1,0:T(8,128)(2,1)S(1)} %param.3), channel_id=1, source_target_pairs={{16,32},{32,16},{48,64},{64,48},{80,96},{96,80},{112,128},{128,112... | collective-permute-start | bytes 786440 | tf_op jit(solution)/shard_map/while/body/eval_jaxpr/cond/branch_1_fun/ppermute | solution.py:275
  287.3 4.8 %collective-permute-done = bf16[4,128,256]{2,1,0:T(8,128)(2,1)} collective-permute-done((bf16[4,128,256]{2,1,0:T(8,128)(2,1)S(1)}, bf16[4,128,256]{2,1,0:T(8,128)(2,1)}, u32[]{:S(2)}, u32[]{:S(2)}) %collective-permute-start) | collective-permute-done | bytes 262176 | tf_op jit(solution)/shard_map/while/body/eval_jaxpr/cond/branch_1_fun/ppermute | solution.py:275
  293.0 11.2 %backward.8 = (bf16[4,128,256]{2,1,0:T(8,128)(2,1)S(1)}, bf16[4,4,128,256]{3,2,1,0:T(8,128)(2,1)}) custom-call(s32[8]{0:T(128)S(1)} %stack.246.flags, bf16[4,128,256]{2,1,0:T(8,128)(2,1)} %get-tuple-element.1676.own, bf16[4,128,256]{2,1,0:T(8,128)(2,1)} %get-tuple-element.1677.outside, ...), custom_call_target="tpu_custom_call", output_to_operand_aliasing={{1}: (19, {})} | custom-call | tf_op jit(solution)/shard_map/while/body/eval_jaxpr/backward/pallas_call | solution.py:491
  304.2 9.9 %conditional.2 = ((bf16[4,128,256]{2,1,0:T(8,128)(2,1)}, bf16[4,128,256]{2,1,0:T(8,128)(2,1)})) conditional(s32[]{:T(128)} %convert_element_type.44, (bf16[4,128,256]{2,1,0:T(8,128)(2,1)}, bf16[4,128,256]{2,1,0:T(8,128)(2,1)}) %tuple.93, bf16[4,128,256]{2,1,0:T(8,128)(2,1)S(1)} %get-tuple-element.1707), branch_computations={%region_3.3_spmd, %region_4.4_spmd} | conditional | bytes 2097256 | solution.py:495
  304.2 5.0 %collective-permute-start = (bf16[4,128,256]{2,1,0:T(8,128)(2,1)S(1)}, bf16[4,128,256]{2,1,0:T(8,128)(2,1)}, u32[]{:S(2)}, u32[]{:S(2)}) collective-permute-start(bf16[4,128,256]{2,1,0:T(8,128)(2,1)S(1)} %param.3), channel_id=1, source_target_pairs={{16,32},{32,16},{48,64},{64,48},{80,96},{96,80},{112,128},{128,112... | collective-permute-start | bytes 786440 | tf_op jit(solution)/shard_map/while/body/eval_jaxpr/cond/branch_1_fun/ppermute | solution.py:275
  309.4 4.8 %collective-permute-done = bf16[4,128,256]{2,1,0:T(8,128)(2,1)} collective-permute-done((bf16[4,128,256]{2,1,0:T(8,128)(2,1)S(1)}, bf16[4,128,256]{2,1,0:T(8,128)(2,1)}, u32[]{:S(2)}, u32[]{:S(2)}) %collective-permute-start) | collective-permute-done | bytes 262176 | tf_op jit(solution)/shard_map/while/body/eval_jaxpr/cond/branch_1_fun/ppermute | solution.py:275
  315.0 12.2 %backward.8 = (bf16[4,128,256]{2,1,0:T(8,128)(2,1)S(1)}, bf16[4,4,128,256]{3,2,1,0:T(8,128)(2,1)}) custom-call(s32[8]{0:T(128)S(1)} %stack.246.flags, bf16[4,128,256]{2,1,0:T(8,128)(2,1)} %get-tuple-element.1676.own, bf16[4,128,256]{2,1,0:T(8,128)(2,1)} %get-tuple-element.1677.outside, ...), custom_call_target="tpu_custom_call", output_to_operand_aliasing={{1}: (19, {})} | custom-call | tf_op jit(solution)/shard_map/while/body/eval_jaxpr/backward/pallas_call | solution.py:491
  329.7 4.2 %collective-permute-start.27 = (bf16[4,128,256]{2,1,0:T(8,128)(2,1)S(1)}, bf16[4,128,256]{2,1,0:T(8,128)(2,1)S(1)}, u32[]{:S(2)}, u32[]{:S(2)}) collective-permute-start(bf16[4,128,256]{2,1,0:T(8,128)(2,1)S(1)} %get-tuple-element.1223), channel_id=1, source_target_pairs={{0,2},{1,3},{2,0},{3,1},{4,6},{5,7},{6,4},{7,5},{8,10},{9,11},{10,... | collective-permute-start | bytes 786440 | tf_op jit(solution)/shard_map/ppermute | solution.py:275
  338.8 2.4 collective-permute-start.25
  341.2 8.0 %collective-permute-done.23 = bf16[4,128,256]{2,1,0:T(8,128)(2,1)S(1)} collective-permute-done((bf16[4,128,256]{2,1,0:T(8,128)(2,1)S(1)}, bf16[4,128,256]{2,1,0:T(8,128)(2,1)S(1)}, u32[]{:S(2)}, u32[]{:S(2)}) %collective-permute-start.23) | collective-permute-done | bytes 262176 | tf_op jit(solution)/shard_map/ppermute | solution.py:275
  349.3 5.9 %collective-permute-done.24 = bf16[4,128,256]{2,1,0:T(8,128)(2,1)S(1)} collective-permute-done((bf16[4,128,256]{2,1,0:T(8,128)(2,1)S(1)}, bf16[4,128,256]{2,1,0:T(8,128)(2,1)S(1)}, u32[]{:S(2)}, u32[]{:S(2)}) %collective-permute-start.24) | collective-permute-done | bytes 262176 | tf_op jit(solution)/shard_map/ppermute | solution.py:275
  (108 shorter events, 38.9 us)
Async XLA Ops:
  0.6 1.3 copy-start
  2.1 10.4 %collective-permute-start.4 = (bf16[304,256]{1,0:T(8,128)(2,1)S(1)}, bf16[304,256]{1,0:T(8,128)(2,1)S(1)}, u32[]{:S(2)}, u32[]{:S(2)}) collective-permute-start(bf16[304,256]{1,0:T(8,128)(2,1)S(1)} %concatenate.14), channel_id=1, source_target_pairs={{0,4},{1,5},{2,6},{3,7},{4,8},{5,9},{6,10},{7,11},{8,12},{9,13},{1... | collective-permute-start | bytes 466952 | tf_op jit(solution)/shard_map/ppermute | solution.py:306
  6.2 46.9 %copy-start.2 = (bf16[4,128,256]{2,1,0:T(8,128)(2,1)}, bf16[4,128,256]{2,1,0:T(8,128)(2,1)S(1)}, u32[]{:S(2)}) copy-start(bf16[4,128,256]{2,1,0:T(8,128)(2,1)S(1)} %get-tuple-element.1645) | copy-start | bytes 786436
  12.5 0.7 copy-start.6
  13.2 51.2 %copy-start.1 = (bf16[10,128,256]{2,1,0:T(8,128)(2,1)}, bf16[10,128,256]{2,1,0:T(8,128)(2,1)S(1)}, u32[]{:S(2)}) copy-start(bf16[10,128,256]{2,1,0:T(8,128)(2,1)S(1)} %after.1) | copy-start | bytes 1966084
  13.2 23.0 %collective-permute-start.5 = (bf16[10,128,256]{2,1,0:T(8,128)(2,1)S(1)}, bf16[10,128,256]{2,1,0:T(8,128)(2,1)}, u32[]{:S(2)}, u32[]{:S(2)}) collective-permute-start(bf16[10,128,256]{2,1,0:T(8,128)(2,1)S(1)} %after.1), channel_id=1, source_target_pairs={{16,32},{32,16},{48,64},{64,48},{80,96},{96,80},{112,128},{128,112... | collective-permute-start | bytes 1966088 | tf_op jit(solution)/shard_map/ppermute | solution.py:275
  19.3 16.8 %collective-permute-start.6 = (bf16[10,128,256]{2,1,0:T(8,128)(2,1)S(1)}, bf16[10,128,256]{2,1,0:T(8,128)(2,1)}, u32[]{:S(2)}, u32[]{:S(2)}) collective-permute-start(bf16[10,128,256]{2,1,0:T(8,128)(2,1)S(1)} %after.1), channel_id=1, source_target_pairs={{0,16},{16,0},{32,48},{48,32},{64,80},{80,64},{96,112},{112,96},{1... | collective-permute-start | bytes 1966088 | tf_op jit(solution)/shard_map/ppermute | solution.py:275
  19.4 10.2 %collective-permute-start.7 = (bf16[304,256]{1,0:T(8,128)(2,1)S(1)}, bf16[304,256]{1,0:T(8,128)(2,1)S(1)}, u32[]{:S(2)}, u32[]{:S(2)}) collective-permute-start(bf16[304,256]{1,0:T(8,128)(2,1)S(1)} %concatenate.14), channel_id=1, source_target_pairs={{0,12},{1,13},{2,14},{3,15},{4,0},{5,1},{6,2},{7,3},{8,4},{9,5},{1... | collective-permute-start | bytes 466952 | tf_op jit(solution)/shard_map/ppermute | solution.py:306
  22.5 10.4 %collective-permute-start.8 = (bf16[152,256]{1,0:T(8,128)(2,1)S(1)}, bf16[152,256]{1,0:T(8,128)(2,1)S(1)}, u32[]{:S(2)}, u32[]{:S(2)}) collective-permute-start(bf16[152,256]{1,0:T(8,128)(2,1)S(1)} %slice.32), channel_id=1, source_target_pairs={{0,4},{1,5},{2,6},{3,7},{4,8},{5,9},{6,10},{7,11},{8,12},{9,13},{1... | collective-permute-start | bytes 233480 | tf_op jit(solution)/shard_map/ppermute | solution.py:306
  29.6 4.7 %collective-permute-start.9 = (bf16[152,256]{1,0:T(8,128)(2,1)S(1)}, bf16[152,256]{1,0:T(8,128)(2,1)S(1)}, u32[]{:S(2)}, u32[]{:S(2)}) collective-permute-start(bf16[152,256]{1,0:T(8,128)(2,1)S(1)} %slice.33), channel_id=1, source_target_pairs={{0,12},{1,13},{2,14},{3,15},{4,0},{5,1},{6,2},{7,3},{8,4},{9,5},{1... | collective-permute-start | bytes 233480 | tf_op jit(solution)/shard_map/ppermute | solution.py:306
  53.2 18.6 %copy-start.3 = (bf16[4,304,256]{2,1,0:T(8,128)(2,1)S(1)}, bf16[4,304,256]{2,1,0:T(8,128)(2,1)}, u32[]{:S(2)}) copy-start(bf16[4,304,256]{2,1,0:T(8,128)(2,1)} %get-tuple-element.1111) | copy-start | bytes 1867780
  53.2 10.0 %collective-permute-start.10 = (bf16[4,304,256]{2,1,0:T(8,128)(2,1)}, bf16[4,304,256]{2,1,0:T(8,128)(2,1)S(1)}, u32[]{:S(2)}, u32[]{:S(2)}) collective-permute-start(bf16[4,304,256]{2,1,0:T(8,128)(2,1)} %get-tuple-element.1111), channel_id=1, source_target_pairs={{0,1},{1,2},{2,3},{3,0},{4,5},{5,6},{6,7},{7,4},{8,9},{9,10},{10,1... | collective-permute-start | bytes 1867784 | tf_op jit(solution)/shard_map/ppermute | solution.py:306
  53.3 11.0 %collective-permute-start.11 = (bf16[4,304,256]{2,1,0:T(8,128)(2,1)}, bf16[4,304,256]{2,1,0:T(8,128)(2,1)S(1)}, u32[]{:S(2)}, u32[]{:S(2)}) collective-permute-start(bf16[4,304,256]{2,1,0:T(8,128)(2,1)} %get-tuple-element.1111), channel_id=1, source_target_pairs={{0,3},{1,0},{2,1},{3,2},{4,7},{5,4},{6,5},{7,6},{8,11},{9,8},{10,9... | collective-permute-start | bytes 1867784 | tf_op jit(solution)/shard_map/ppermute | solution.py:306
  63.2 5.8 %collective-permute-start.12 = (bf16[2,304,256]{2,1,0:T(8,128)(2,1)S(1)}, bf16[2,304,256]{2,1,0:T(8,128)(2,1)S(1)}, u32[]{:S(2)}, u32[]{:S(2)}) collective-permute-start(bf16[2,304,256]{2,1,0:T(8,128)(2,1)S(1)} %slice.34), channel_id=1, source_target_pairs={{0,1},{1,2},{2,3},{3,0},{4,5},{5,6},{6,7},{7,4},{8,9},{9,10},{10,1... | collective-permute-start | bytes 933896 | tf_op jit(solution)/shard_map/ppermute | solution.py:306
  64.3 7.3 %collective-permute-start.13 = (bf16[2,304,256]{2,1,0:T(8,128)(2,1)S(1)}, bf16[2,304,256]{2,1,0:T(8,128)(2,1)S(1)}, u32[]{:S(2)}, u32[]{:S(2)}) collective-permute-start(bf16[2,304,256]{2,1,0:T(8,128)(2,1)S(1)} %slice.35), channel_id=1, source_target_pairs={{0,3},{1,0},{2,1},{3,2},{4,7},{5,4},{6,5},{7,6},{8,11},{9,8},{10,9... | collective-permute-start | bytes 933896 | tf_op jit(solution)/shard_map/ppermute | solution.py:306
  73.5 30.9 %collective-permute-start.14 = (bf16[4,4,304,256]{3,2,1,0:T(8,128)(2,1)}, bf16[4,4,304,256]{3,2,1,0:T(8,128)(2,1)}, u32[]{:S(2)}, u32[]{:S(2)}) collective-permute-start(bf16[4,4,304,256]{3,2,1,0:T(8,128)(2,1)} %pad_maximum_fusion), channel_id=1, source_target_pairs={{0,32},{1,33},{2,34},{3,35},{4,36},{5,37},{6,38},{7,39},{8,40},{9,... | collective-permute-start | bytes 7471112 | tf_op jit(solution)/shard_map/ppermute | solution.py:306
  74.2 31.8 %collective-permute-start.15 = (bf16[4,4,304,256]{3,2,1,0:T(8,128)(2,1)}, bf16[4,4,304,256]{3,2,1,0:T(8,128)(2,1)}, u32[]{:S(2)}, u32[]{:S(2)}) collective-permute-start(bf16[4,4,304,256]{3,2,1,0:T(8,128)(2,1)} %pad_maximum_fusion), channel_id=1, source_target_pairs={{0,96},{1,97},{2,98},{3,99},{4,100},{5,101},{6,102},{7,103},{8,104... | collective-permute-start | bytes 7471112 | tf_op jit(solution)/shard_map/ppermute | solution.py:306
  76.2 55.3 %collective-permute-start.18 = (bf16[4,4,304,256]{3,2,1,0:T(8,128)(2,1)}, bf16[4,4,304,256]{3,2,1,0:T(8,128)(2,1)}, u32[]{:S(2)}, u32[]{:S(2)}) collective-permute-start(bf16[4,4,304,256]{3,2,1,0:T(8,128)(2,1)} %pad_maximum_fusion), channel_id=1, source_target_pairs={{0,16},{1,17},{2,18},{3,19},{4,20},{5,21},{6,22},{7,23},{8,24},{9,... | collective-permute-start | bytes 7471112 | tf_op jit(solution)/shard_map/ppermute | solution.py:306
  105.8 17.4 %collective-permute-start.16 = (bf16[2,4,304,256]{3,2,1,0:T(8,128)(2,1)S(1)}, bf16[2,4,304,256]{3,2,1,0:T(8,128)(2,1)}, u32[]{:S(2)}, u32[]{:S(2)}) collective-permute-start(bf16[2,4,304,256]{3,2,1,0:T(8,128)(2,1)S(1)} %slice.36), channel_id=1, source_target_pairs={{0,32},{1,33},{2,34},{3,35},{4,36},{5,37},{6,38},{7,39},{8,40},{9,... | collective-permute-start | bytes 3735560 | tf_op jit(solution)/shard_map/ppermute | solution.py:306
  107.3 18.9 %collective-permute-start.17 = (bf16[2,4,304,256]{3,2,1,0:T(8,128)(2,1)S(1)}, bf16[2,4,304,256]{3,2,1,0:T(8,128)(2,1)}, u32[]{:S(2)}, u32[]{:S(2)}) collective-permute-start(bf16[2,4,304,256]{3,2,1,0:T(8,128)(2,1)S(1)} %slice.37), channel_id=1, source_target_pairs={{0,96},{1,97},{2,98},{3,99},{4,100},{5,101},{6,102},{7,103},{8,104... | collective-permute-start | bytes 3735560 | tf_op jit(solution)/shard_map/ppermute | solution.py:306
  110.1 24.3 %collective-permute-start.19 = (bf16[4,4,304,256]{3,2,1,0:T(8,128)(2,1)}, bf16[4,4,304,256]{3,2,1,0:T(8,128)(2,1)}, u32[]{:S(2)}, u32[]{:S(2)}) collective-permute-start(bf16[4,4,304,256]{3,2,1,0:T(8,128)(2,1)} %collective-permute-done.14), channel_id=1, source_target_pairs={{0,16},{1,17},{2,18},{3,19},{4,20},{5,21},{6,22},{7,23},{8,24},{9,... | collective-permute-start | bytes 7471112 | tf_op jit(solution)/shard_map/ppermute | solution.py:306
  113.4 21.0 %collective-permute-start.20 = (bf16[4,4,304,256]{3,2,1,0:T(8,128)(2,1)}, bf16[4,4,304,256]{3,2,1,0:T(8,128)(2,1)}, u32[]{:S(2)}, u32[]{:S(2)}) collective-permute-start(bf16[4,4,304,256]{3,2,1,0:T(8,128)(2,1)} %collective-permute-done.15), channel_id=1, source_target_pairs={{0,16},{1,17},{2,18},{3,19},{4,20},{5,21},{6,22},{7,23},{8,24},{9,... | collective-permute-start | bytes 7471112 | tf_op jit(solution)/shard_map/ppermute | solution.py:306
  123.3 8.2 %collective-permute-start.21 = (bf16[2,4,304,256]{3,2,1,0:T(8,128)(2,1)}, bf16[2,4,304,256]{3,2,1,0:T(8,128)(2,1)}, u32[]{:S(2)}, u32[]{:S(2)}) collective-permute-start(bf16[2,4,304,256]{3,2,1,0:T(8,128)(2,1)} %collective-permute-done.16), channel_id=1, source_target_pairs={{0,16},{1,17},{2,18},{3,19},{4,20},{5,21},{6,22},{7,23},{8,24},{9,... | collective-permute-start | bytes 3735560 | tf_op jit(solution)/shard_map/ppermute | solution.py:306
  126.2 8.2 %collective-permute-start.22 = (bf16[2,4,304,256]{3,2,1,0:T(8,128)(2,1)}, bf16[2,4,304,256]{3,2,1,0:T(8,128)(2,1)}, u32[]{:S(2)}, u32[]{:S(2)}) collective-permute-start(bf16[2,4,304,256]{3,2,1,0:T(8,128)(2,1)} %collective-permute-done.17), channel_id=1, source_target_pairs={{0,16},{1,17},{2,18},{3,19},{4,20},{5,21},{6,22},{7,23},{8,24},{9,... | collective-permute-start | bytes 3735560 | tf_op jit(solution)/shard_map/ppermute | solution.py:306
  146.8 23.4 %collective-permute-start.2 = (bf16[10,128,256]{2,1,0:T(8,128)(2,1)S(1)}, bf16[10,128,256]{2,1,0:T(8,128)(2,1)}, u32[]{:S(2)}, u32[]{:S(2)}) collective-permute-start(bf16[10,128,256]{2,1,0:T(8,128)(2,1)S(1)} %get-tuple-element.1616), channel_id=1, source_target_pairs={{16,32},{32,16},{48,64},{64,48},{80,96},{96,80},{112,128},{128,112... | collective-permute-start | bytes 1966088 | tf_op jit(solution)/shard_map/while/body/eval_jaxpr/ppermute | solution.py:275
  161.9 8.4 %collective-permute-start.3 = (bf16[10,128,256]{2,1,0:T(8,128)(2,1)S(1)}, bf16[10,128,256]{2,1,0:T(8,128)(2,1)}, u32[]{:S(2)}, u32[]{:S(2)}) collective-permute-start(bf16[10,128,256]{2,1,0:T(8,128)(2,1)S(1)} %get-tuple-element.1616), channel_id=1, source_target_pairs={{0,16},{16,0},{32,48},{48,32},{64,80},{80,64},{96,112},{112,96},{1... | collective-permute-start | bytes 1966088 | tf_op jit(solution)/shard_map/while/body/eval_jaxpr/ppermute | solution.py:275
  182.3 14.1 %collective-permute-start.2 = (bf16[10,128,256]{2,1,0:T(8,128)(2,1)S(1)}, bf16[10,128,256]{2,1,0:T(8,128)(2,1)}, u32[]{:S(2)}, u32[]{:S(2)}) collective-permute-start(bf16[10,128,256]{2,1,0:T(8,128)(2,1)S(1)} %get-tuple-element.1616), channel_id=1, source_target_pairs={{16,32},{32,16},{48,64},{64,48},{80,96},{96,80},{112,128},{128,112... | collective-permute-start | bytes 1966088 | tf_op jit(solution)/shard_map/while/body/eval_jaxpr/ppermute | solution.py:275
  187.8 8.6 %collective-permute-start.3 = (bf16[10,128,256]{2,1,0:T(8,128)(2,1)S(1)}, bf16[10,128,256]{2,1,0:T(8,128)(2,1)}, u32[]{:S(2)}, u32[]{:S(2)}) collective-permute-start(bf16[10,128,256]{2,1,0:T(8,128)(2,1)S(1)} %get-tuple-element.1616), channel_id=1, source_target_pairs={{0,16},{16,0},{32,48},{48,32},{64,80},{80,64},{96,112},{112,96},{1... | collective-permute-start | bytes 1966088 | tf_op jit(solution)/shard_map/while/body/eval_jaxpr/ppermute | solution.py:275
  208.5 14.1 %collective-permute-start.2 = (bf16[10,128,256]{2,1,0:T(8,128)(2,1)S(1)}, bf16[10,128,256]{2,1,0:T(8,128)(2,1)}, u32[]{:S(2)}, u32[]{:S(2)}) collective-permute-start(bf16[10,128,256]{2,1,0:T(8,128)(2,1)S(1)} %get-tuple-element.1616), channel_id=1, source_target_pairs={{16,32},{32,16},{48,64},{64,48},{80,96},{96,80},{112,128},{128,112... | collective-permute-start | bytes 1966088 | tf_op jit(solution)/shard_map/while/body/eval_jaxpr/ppermute | solution.py:275
  213.8 8.8 %collective-permute-start.3 = (bf16[10,128,256]{2,1,0:T(8,128)(2,1)S(1)}, bf16[10,128,256]{2,1,0:T(8,128)(2,1)}, u32[]{:S(2)}, u32[]{:S(2)}) collective-permute-start(bf16[10,128,256]{2,1,0:T(8,128)(2,1)S(1)} %get-tuple-element.1616), channel_id=1, source_target_pairs={{0,16},{16,0},{32,48},{48,32},{64,80},{80,64},{96,112},{112,96},{1... | collective-permute-start | bytes 1966088 | tf_op jit(solution)/shard_map/while/body/eval_jaxpr/ppermute | solution.py:275
  234.7 14.1 %collective-permute-start.2 = (bf16[10,128,256]{2,1,0:T(8,128)(2,1)S(1)}, bf16[10,128,256]{2,1,0:T(8,128)(2,1)}, u32[]{:S(2)}, u32[]{:S(2)}) collective-permute-start(bf16[10,128,256]{2,1,0:T(8,128)(2,1)S(1)} %get-tuple-element.1616), channel_id=1, source_target_pairs={{16,32},{32,16},{48,64},{64,48},{80,96},{96,80},{112,128},{128,112... | collective-permute-start | bytes 1966088 | tf_op jit(solution)/shard_map/while/body/eval_jaxpr/ppermute | solution.py:275
  239.7 9.1 %collective-permute-start.3 = (bf16[10,128,256]{2,1,0:T(8,128)(2,1)S(1)}, bf16[10,128,256]{2,1,0:T(8,128)(2,1)}, u32[]{:S(2)}, u32[]{:S(2)}) collective-permute-start(bf16[10,128,256]{2,1,0:T(8,128)(2,1)S(1)} %get-tuple-element.1616), channel_id=1, source_target_pairs={{0,16},{16,0},{32,48},{48,32},{64,80},{80,64},{96,112},{112,96},{1... | collective-permute-start | bytes 1966088 | tf_op jit(solution)/shard_map/while/body/eval_jaxpr/ppermute | solution.py:275
  260.3 9.9 %collective-permute-start = (bf16[4,128,256]{2,1,0:T(8,128)(2,1)S(1)}, bf16[4,128,256]{2,1,0:T(8,128)(2,1)}, u32[]{:S(2)}, u32[]{:S(2)}) collective-permute-start(bf16[4,128,256]{2,1,0:T(8,128)(2,1)S(1)} %param.3), channel_id=1, source_target_pairs={{16,32},{32,16},{48,64},{64,48},{80,96},{96,80},{112,128},{128,112... | collective-permute-start | bytes 786440 | tf_op jit(solution)/shard_map/while/body/eval_jaxpr/cond/branch_1_fun/ppermute | solution.py:275
  265.2 5.0 %collective-permute-start.1 = (bf16[4,128,256]{2,1,0:T(8,128)(2,1)S(1)}, bf16[4,128,256]{2,1,0:T(8,128)(2,1)}, u32[]{:S(2)}, u32[]{:S(2)}) collective-permute-start(bf16[4,128,256]{2,1,0:T(8,128)(2,1)S(1)} %param.3), channel_id=1, source_target_pairs={{0,16},{16,0},{32,48},{48,32},{64,80},{80,64},{96,112},{112,96},{1... | collective-permute-start | bytes 786440 | tf_op jit(solution)/shard_map/while/body/eval_jaxpr/cond/branch_1_fun/ppermute | solution.py:275
  282.3 9.9 %collective-permute-start = (bf16[4,128,256]{2,1,0:T(8,128)(2,1)S(1)}, bf16[4,128,256]{2,1,0:T(8,128)(2,1)}, u32[]{:S(2)}, u32[]{:S(2)}) collective-permute-start(bf16[4,128,256]{2,1,0:T(8,128)(2,1)S(1)} %param.3), channel_id=1, source_target_pairs={{16,32},{32,16},{48,64},{64,48},{80,96},{96,80},{112,128},{128,112... | collective-permute-start | bytes 786440 | tf_op jit(solution)/shard_map/while/body/eval_jaxpr/cond/branch_1_fun/ppermute | solution.py:275
  287.2 4.9 %collective-permute-start.1 = (bf16[4,128,256]{2,1,0:T(8,128)(2,1)S(1)}, bf16[4,128,256]{2,1,0:T(8,128)(2,1)}, u32[]{:S(2)}, u32[]{:S(2)}) collective-permute-start(bf16[4,128,256]{2,1,0:T(8,128)(2,1)S(1)} %param.3), channel_id=1, source_target_pairs={{0,16},{16,0},{32,48},{48,32},{64,80},{80,64},{96,112},{112,96},{1... | collective-permute-start | bytes 786440 | tf_op jit(solution)/shard_map/while/body/eval_jaxpr/cond/branch_1_fun/ppermute | solution.py:275
  304.2 9.9 %collective-permute-start = (bf16[4,128,256]{2,1,0:T(8,128)(2,1)S(1)}, bf16[4,128,256]{2,1,0:T(8,128)(2,1)}, u32[]{:S(2)}, u32[]{:S(2)}) collective-permute-start(bf16[4,128,256]{2,1,0:T(8,128)(2,1)S(1)} %param.3), channel_id=1, source_target_pairs={{16,32},{32,16},{48,64},{64,48},{80,96},{96,80},{112,128},{128,112... | collective-permute-start | bytes 786440 | tf_op jit(solution)/shard_map/while/body/eval_jaxpr/cond/branch_1_fun/ppermute | solution.py:275
  309.3 4.9 %collective-permute-start.1 = (bf16[4,128,256]{2,1,0:T(8,128)(2,1)S(1)}, bf16[4,128,256]{2,1,0:T(8,128)(2,1)}, u32[]{:S(2)}, u32[]{:S(2)}) collective-permute-start(bf16[4,128,256]{2,1,0:T(8,128)(2,1)S(1)} %param.3), channel_id=1, source_target_pairs={{0,16},{16,0},{32,48},{48,32},{64,80},{80,64},{96,112},{112,96},{1... | collective-permute-start | bytes 786440 | tf_op jit(solution)/shard_map/while/body/eval_jaxpr/cond/branch_1_fun/ppermute | solution.py:275
  329.1 9.7 %collective-permute-start.26 = (bf16[4,128,256]{2,1,0:T(8,128)(2,1)S(1)}, bf16[4,128,256]{2,1,0:T(8,128)(2,1)S(1)}, u32[]{:S(2)}, u32[]{:S(2)}) collective-permute-start(bf16[4,128,256]{2,1,0:T(8,128)(2,1)S(1)} %get-tuple-element.1224), channel_id=1, source_target_pairs={{0,1},{1,2},{2,3},{3,0},{4,5},{5,6},{6,7},{7,4},{8,9},{9,10},{10,1... | collective-permute-start | bytes 786440 | tf_op jit(solution)/shard_map/ppermute | solution.py:275
  329.7 19.6 %collective-permute-start.27 = (bf16[4,128,256]{2,1,0:T(8,128)(2,1)S(1)}, bf16[4,128,256]{2,1,0:T(8,128)(2,1)S(1)}, u32[]{:S(2)}, u32[]{:S(2)}) collective-permute-start(bf16[4,128,256]{2,1,0:T(8,128)(2,1)S(1)} %get-tuple-element.1223), channel_id=1, source_target_pairs={{0,2},{1,3},{2,0},{3,1},{4,6},{5,7},{6,4},{7,5},{8,10},{9,11},{10,... | collective-permute-start | bytes 786440 | tf_op jit(solution)/shard_map/ppermute | solution.py:275
  333.8 21.4 %collective-permute-start.28 = (bf16[4,128,256]{2,1,0:T(8,128)(2,1)S(1)}, bf16[4,128,256]{2,1,0:T(8,128)(2,1)S(1)}, u32[]{:S(2)}, u32[]{:S(2)}) collective-permute-start(bf16[4,128,256]{2,1,0:T(8,128)(2,1)S(1)} %get-tuple-element.1222), channel_id=1, source_target_pairs={{0,3},{1,0},{2,1},{3,2},{4,7},{5,4},{6,5},{7,6},{8,11},{9,8},{10,9... | collective-permute-start | bytes 786440 | tf_op jit(solution)/shard_map/ppermute | solution.py:275
  335.0 14.2 %collective-permute-start.23 = (bf16[4,128,256]{2,1,0:T(8,128)(2,1)S(1)}, bf16[4,128,256]{2,1,0:T(8,128)(2,1)S(1)}, u32[]{:S(2)}, u32[]{:S(2)}) collective-permute-start(bf16[4,128,256]{2,1,0:T(8,128)(2,1)S(1)} %get-tuple-element.1227), channel_id=1, source_target_pairs={{0,1},{1,2},{2,3},{3,0},{4,5},{5,6},{6,7},{7,4},{8,9},{9,10},{10,1... | collective-permute-start | bytes 786440 | tf_op jit(solution)/shard_map/ppermute | solution.py:275
  338.7 16.5 %collective-permute-start.24 = (bf16[4,128,256]{2,1,0:T(8,128)(2,1)S(1)}, bf16[4,128,256]{2,1,0:T(8,128)(2,1)S(1)}, u32[]{:S(2)}, u32[]{:S(2)}) collective-permute-start(bf16[4,128,256]{2,1,0:T(8,128)(2,1)S(1)} %get-tuple-element.1226), channel_id=1, source_target_pairs={{0,2},{1,3},{2,0},{3,1},{4,6},{5,7},{6,4},{7,5},{8,10},{9,11},{10,... | collective-permute-start | bytes 786440 | tf_op jit(solution)/shard_map/ppermute | solution.py:275
  338.8 16.4 %collective-permute-start.25 = (bf16[4,128,256]{2,1,0:T(8,128)(2,1)S(1)}, bf16[4,128,256]{2,1,0:T(8,128)(2,1)S(1)}, u32[]{:S(2)}, u32[]{:S(2)}) collective-permute-start(bf16[4,128,256]{2,1,0:T(8,128)(2,1)S(1)} %get-tuple-element.1225), channel_id=1, source_target_pairs={{0,3},{1,0},{2,1},{3,2},{4,7},{5,4},{6,5},{7,6},{8,11},{9,8},{10,9... | collective-permute-start | bytes 786440 | tf_op jit(solution)/shard_map/ppermute | solution.py:275
  355.2 1.0 copy-start.5
  356.2 1.0 copy-start.4
where the time goes:
time: 359 us; the launch traced here: 357 us
  waiting for transfers between devices  126 us (35%)
  Pallas kernels  111 us (31%)
  starting transfers between devices  93.3 us (26%)
  local copies, waits for them, and re-layouts  20.7 us (6%)
  other arithmetic  4.56 us (1%)
    ppermute x17, waiting for transfers between devices, carry(): return lax.ppermute(block, ('band', 'section'), pairs)  66.8 us
    ppermute x22, starting transfers between devices, shift(): return lax.ppermute(block, axis, pairs)  61.4 us
    ppermute x22, waiting for transfers between devices, shift(): return lax.ppermute(block, axis, pairs)  59.3 us
    pallas_call x4, Pallas kernels, forward_step(): forward(flags_of(block), edge, outside, inside, *mine, *theirs, *kept)  48.2 us
    pallas_call x4, Pallas kernels, backward_step(): backward(flags_of(block), upstream, above, below, slopes, far_outside, fa...  46 us
    ppermute x17, starting transfers between devices, carry(): return lax.ppermute(block, ('band', 'section'), pairs)  31.9 us
    pallas_call x1, Pallas kernels, on_device(): pl.pallas_call(take_edges, out_shape=(jax.ShapeDtypeStruct(piece.shape, B...  17 us
  transfers between devices with their start and end apart: 39, of which 19 were waited for; matrix products, arithmetic and copies ran while one was open for 4% of the time, Pallas kernels for 0%

commit v1 on v0

--- a/solution.py
+++ b/solution.py
@@ -329,42 +329,21 @@
     piece = lax.dynamic_slice_in_dim(kernels.reshape(9 * channels, channels), start, quarter, 0)
     piece = jnp.concatenate([piece, extra])
     hbm = pl.BlockSpec(memory_space=pl.ANY)
-
-    def after(block, *others):
-        return pl.pallas_call(
-            lambda *refs: None,
-            out_shape=jax.ShapeDtypeStruct(block.shape, BF16),
-            in_specs=[hbm] * (1 + len(others)),
-            out_specs=hbm,
-            input_output_aliases={0: 0},
-            name="after",
-        )(block, *others)
-
-    forth, back = route(lambda y, c, z, x: (y, c, z + 1, x)), route(lambda y, c, z, x: (y, c, z - 1, x))
-    behind, ahead = carry(piece, forth), carry(piece, back)
-    low, high = carry(behind[: (quarter + EXTRA) // 2], forth), carry(ahead[(quarter + EXTRA) // 2 :], back)
-    edge = after(edge, behind)
+    vmem = pl.BlockSpec(memory_space=pltpu.VMEM)
     edge_outside, edge_inside = edges(edge)
-
-    def take_edges(piece, outside, inside, out, first, second, sems):
-        copies = [
-            pltpu.make_async_copy(source.at[pl.ds(rows, rows)], target, sems.at[index])
-            for index, (source, target) in enumerate(((outside, first), (inside, second)))
-        ]
-        for copy in copies:
-            copy.start()
-        for copy in copies:
-            copy.wait()
-
-    piece = jnp.stack([piece, behind, ahead, jnp.concatenate([low, high])])
+    piece = joined(piece, lambda y, c, z, x: (y, c, z + 1, x), lambda y, c, z, x: (y, c, z - 1, x))
+
+    def take_edges(piece, outside, inside, out, first, second):
+        first[...] = outside[rows : 2 * rows]
+        second[...] = inside[rows : 2 * rows]
+
     part_shape = jax.ShapeDtypeStruct((rows, across, channels), BF16)
     piece, start_outside, start_inside = pl.pallas_call(
         take_edges,
         out_shape=(jax.ShapeDtypeStruct(piece.shape, BF16), part_shape, part_shape),
-        in_specs=[hbm] * 3,
-        out_specs=(hbm,) * 3,
+        in_specs=[hbm, vmem, vmem],
+        out_specs=(hbm, vmem, vmem),
         input_output_aliases={0: 0},
-        scratch_shapes=[pltpu.SemaphoreType.DMA((2,))],
         name="take_edges",
     )(piece, edge_outside, edge_inside)
     piece = joined(
@@ -473,17 +452,30 @@
         0, groups, forward_step, state
     )
 
-    def deliver(kept):
-        out = jnp.zeros((micro_count,) + row_shape, BF16)
-        out = lax.dynamic_update_index_in_dim(out, lax.dynamic_index_in_dim(kept, place, 0, keepdims=False), place, 0)
+    def sent(kept):
+        received = [lax.dynamic_index_in_dim(kept, place, 0, keepdims=False)]
         for step in range(1, DEPTH):
             send = lax.dynamic_index_in_dim(kept, (place + step) % DEPTH, 0, keepdims=False)
             pairs = [(g * DEPTH + p, g * DEPTH + (p + step) % DEPTH) for g in range(groups) for p in range(DEPTH)]
-            received = shift(send, "section", pairs)
-            out = lax.dynamic_update_index_in_dim(out, received, (place - step) % DEPTH, 0)
-        return out[None]
-
-    delivered = deliver(states)
+            received.append(shift(send, "section", pairs))
+        return received
+
+    def set_in_order(places, *refs):
+        out = refs[-1]
+        for index, piece in enumerate(refs[:-1]):
+            out[places[index]] = piece[...]
+
+    def in_order(received):
+        places = jnp.stack([(place - step) % DEPTH for step in range(DEPTH)]).astype(jnp.int32)
+        return pl.pallas_call(
+            set_in_order,
+            out_shape=shaped(micro_count, *row_shape),
+            in_specs=[smem] + [vmem] * DEPTH,
+            out_specs=vmem,
+            name="set_in_order",
+        )(places, *received)[None]
+
+    received = sent(states)
 
     def backward_step(step, state):
         upstream, above, below, grads = state
@@ -498,7 +490,7 @@
     state = (upstream, start_outside, start_inside, room[4])
     grads = lax.fori_loop(0, groups, backward_step, state)[3]
 
-    return delivered, deliver(grads)
+    return in_order(received), in_order(sent(grads))
 
 
 def solution(mesh):

time: 359 us -> 334 us (0.930)
  starting transfers between devices: 93.3 us -> 74.5 us
  Pallas kernels: 111 us -> 101 us
  waiting for transfers between devices: 126 us -> 136 us
  local copies, waits for them, and re-layouts: 20.7 us -> 16.7 us
    pallas_call x1, Pallas kernels: 17 us -> 2.1 us  [on_device(): pl.pallas_call(take_edges, out_shape=(jax.ShapeDtypeStruct(piece.shape, B...]
    ppermute x17, starting transfers between devices: 31.9 us -> 18.5 us  [carry(): return lax.ppermute(block, ('band', 'section'), pairs)]
    ppermute x17, waiting for transfers between devices: 66.8 us -> 78.3 us  [carry(): return lax.ppermute(block, ('band', 'section'), pairs)]
    ppermute x22, starting transfers between devices: 61.4 us -> 56 us  [shift(): return lax.ppermute(block, axis, pairs)]
    pallas_call x1 -> x2, Pallas kernels: 0.01 us -> 4.47 us  [in_order(): pl.pallas_call(set_in_order, out_shape=shaped(micro_count, *row_shape), i...]
  transfers between devices with their start and end apart: 39 -> 39, of which waited for: 19 -> 21; matrix products, arithmetic and copies ran while one was open for 4% -> 3% of each run, Pallas kernels for 0% -> 1%
where the time goes in v1:
time: 334 us; the launch traced here: 332 us
  waiting for transfers between devices  136 us (41%)
  Pallas kernels  101 us (30%)
  starting transfers between devices  74.5 us (22%)
  local copies, waits for them, and re-layouts  16.7 us (5%)
  other arithmetic  3.55 us (1%)
    ppermute x17, waiting for transfers between devices, carry(): return lax.ppermute(block, ('band', 'section'), pairs)  78.3 us
    ppermute x22, waiting for transfers between devices, shift(): return lax.ppermute(block, axis, pairs)  57.5 us
    ppermute x22, starting transfers between devices, shift(): return lax.ppermute(block, axis, pairs)  56 us
    pallas_call x4, Pallas kernels, forward_step(): forward(flags_of(block), edge, outside, inside, *mine, *theirs, *kept)  48.2 us
    pallas_call x4, Pallas kernels, backward_step(): backward(flags_of(block), upstream, above, below, slopes, far_outside, fa...  46 us
    ppermute x17, starting transfers between devices, carry(): return lax.ppermute(block, ('band', 'section'), pairs)  18.5 us
  transfers between devices with their start and end apart: 39, of which 21 were waited for; matrix products, arithmetic and copies ran while one was open for 3% of the time, Pallas kernels for 1%

profile of v1, /device:TPU:25, one launch (start us, length us, event | category | flops | bytes accessed | tf_op | source)
XLA Modules:
  0.0 332.5 jit_solution(241462693264549537)
XLA Ops:
  2.9 3.8 %collective-permute-start.4 = (bf16[10,128,256]{2,1,0:T(8,128)(2,1)S(1)}, bf16[10,128,256]{2,1,0:T(8,128)(2,1)}, u32[]{:S(2)}, u32[]{:S(2)}) collective-permute-start(bf16[10,128,256]{2,1,0:T(8,128)(2,1)S(1)} %pad_maximum_fusion.1), channel_id=1, source_target_pairs={{16,32},{32,16},{48,64},{64,48},{80,96},{96,80},{112,128},{128,112... | collective-permute-start | bytes 1966088 | tf_op jit(solution)/shard_map/ppermute | solution.py:275
  7.0 3.1 collective-permute-start.6
  10.1 2.2 collective-permute-start.7
  12.3 16.6 %collective-permute-done.6 = bf16[304,256]{1,0:T(8,128)(2,1)S(1)} collective-permute-done((bf16[304,256]{1,0:T(8,128)(2,1)S(1)}, bf16[304,256]{1,0:T(8,128)(2,1)S(1)}, u32[]{:S(2)}, u32[]{:S(2)}) %collective-permute-start.6) | collective-permute-done | bytes 155680 | tf_op jit(solution)/shard_map/ppermute | solution.py:306
  28.9 3.6 %collective-permute-start.9 = (bf16[152,256]{1,0:T(8,128)(2,1)S(1)}, bf16[152,256]{1,0:T(8,128)(2,1)S(1)}, u32[]{:S(2)}, u32[]{:S(2)}) collective-permute-start(bf16[152,256]{1,0:T(8,128)(2,1)S(1)} %slice.33), channel_id=1, source_target_pairs={{0,12},{1,13},{2,14},{3,15},{4,0},{5,1},{6,2},{7,3},{8,4},{9,5},{1... | collective-permute-start | bytes 233480 | tf_op jit(solution)/shard_map/ppermute | solution.py:306
  35.2 2.1 take_edges.1
  38.8 7.8 %collective-permute-done.10 = bf16[4,304,256]{2,1,0:T(8,128)(2,1)S(1)} collective-permute-done((bf16[4,304,256]{2,1,0:T(8,128)(2,1)}, bf16[4,304,256]{2,1,0:T(8,128)(2,1)S(1)}, u32[]{:S(2)}, u32[]{:S(2)}) %collective-permute-start.10) | collective-permute-done | bytes 622624 | tf_op jit(solution)/shard_map/ppermute | solution.py:306
  48.4 4.0 %collective-permute-done.12 = bf16[2,304,256]{2,1,0:T(8,128)(2,1)S(1)} collective-permute-done((bf16[2,304,256]{2,1,0:T(8,128)(2,1)S(1)}, bf16[2,304,256]{2,1,0:T(8,128)(2,1)S(1)}, u32[]{:S(2)}, u32[]{:S(2)}) %collective-permute-start.12) | collective-permute-done | bytes 311328 | tf_op jit(solution)/shard_map/ppermute | solution.py:306
  52.4 2.8 collective-permute-done.13
  55.3 1.8 pad_maximum_fusion
  59.8 27.9 %collective-permute-done.14 = bf16[4,4,304,256]{3,2,1,0:T(8,128)(2,1)} collective-permute-done((bf16[4,4,304,256]{3,2,1,0:T(8,128)(2,1)}, bf16[4,4,304,256]{3,2,1,0:T(8,128)(2,1)}, u32[]{:S(2)}, u32[]{:S(2)}) %collective-permute-start.14) | collective-permute-done | bytes 2490400 | tf_op jit(solution)/shard_map/ppermute | solution.py:306
  90.6 2.7 collective-permute-start.17
  93.9 12.7 %collective-permute-done.16 = bf16[2,4,304,256]{3,2,1,0:T(8,128)(2,1)} collective-permute-done((bf16[2,4,304,256]{3,2,1,0:T(8,128)(2,1)S(1)}, bf16[2,4,304,256]{3,2,1,0:T(8,128)(2,1)}, u32[]{:S(2)}, u32[]{:S(2)}) %collective-permute-start.16) | collective-permute-done | bytes 1245216 | tf_op jit(solution)/shard_map/ppermute | solution.py:306
  107.7 2.1 collective-permute-done.21
  111.7 110.6 %while.48 = (s32[]{:T(128)}, bf16[10,128,256]{2,1,0:T(8,128)(2,1)}, bf16[10,128,256]{2,1,0:T(8,128)(2,1)}, bf16[10,128,256]{2,1,0:T(8,128)(2,1)}, bf16[4,28,128,...) while((s32[]{:T(128)}, bf16[10,128,256]{2,1,0:T(8,128)(2,1)}, ...), condition=%wide.region_1.2_spmd, body=%wide.region_0.1_spmd.sunk | while | flops 20 | bytes 6554172 | solution.py:451
  111.7 12.3 %forward.8 = (bf16[10,128,256]{2,1,0:T(8,128)(2,1)S(1)}, bf16[4,28,128,256]{3,2,1,0:T(8,128)(2,1)}, bf16[4,4,128,256]{3,2,1,0:T(8,128)(2,1)}, bf16[4,6,128,256]{...) custom-call(s32[8]{0:T(128)S(1)} %stack.268.flags, ...), custom_call_target="tpu_custom_call", output_to_operand_aliasing={{1}: (14, {}), {2}: (15, {}), {3}: (16, {}), {4}: (17, {})} | custom-call | tf_op jit(solution)/shard_map/while/body/eval_jaxpr/forward/pallas_call | solution.py:435
  124.1 11.2 %collective-permute-start.2 = (bf16[10,128,256]{2,1,0:T(8,128)(2,1)S(1)}, bf16[10,128,256]{2,1,0:T(8,128)(2,1)}, u32[]{:S(2)}, u32[]{:S(2)}) collective-permute-start(bf16[10,128,256]{2,1,0:T(8,128)(2,1)S(1)} %get-tuple-element.1618), channel_id=1, source_target_pairs={{16,32},{32,16},{48,64},{64,48},{80,96},{96,80},{112,128},{128,112... | collective-permute-start | bytes 1966088 | tf_op jit(solution)/shard_map/while/body/eval_jaxpr/ppermute | solution.py:275
  136.3 7.4 %collective-permute-done.2 = bf16[10,128,256]{2,1,0:T(8,128)(2,1)} collective-permute-done((bf16[10,128,256]{2,1,0:T(8,128)(2,1)S(1)}, bf16[10,128,256]{2,1,0:T(8,128)(2,1)}, u32[]{:S(2)}, u32[]{:S(2)}) %collective-permute-start.2) | collective-permute-done | bytes 655392 | tf_op jit(solution)/shard_map/while/body/eval_jaxpr/ppermute | solution.py:275
  143.8 12.0 %forward.8 = (bf16[10,128,256]{2,1,0:T(8,128)(2,1)S(1)}, bf16[4,28,128,256]{3,2,1,0:T(8,128)(2,1)}, bf16[4,4,128,256]{3,2,1,0:T(8,128)(2,1)}, bf16[4,6,128,256]{...) custom-call(s32[8]{0:T(128)S(1)} %stack.268.flags, ...), custom_call_target="tpu_custom_call", output_to_operand_aliasing={{1}: (14, {}), {2}: (15, {}), {3}: (16, {}), {4}: (17, {})} | custom-call | tf_op jit(solution)/shard_map/while/body/eval_jaxpr/forward/pallas_call | solution.py:435
  155.7 5.5 %collective-permute-start.2 = (bf16[10,128,256]{2,1,0:T(8,128)(2,1)S(1)}, bf16[10,128,256]{2,1,0:T(8,128)(2,1)}, u32[]{:S(2)}, u32[]{:S(2)}) collective-permute-start(bf16[10,128,256]{2,1,0:T(8,128)(2,1)S(1)} %get-tuple-element.1618), channel_id=1, source_target_pairs={{16,32},{32,16},{48,64},{64,48},{80,96},{96,80},{112,128},{128,112... | collective-permute-start | bytes 1966088 | tf_op jit(solution)/shard_map/while/body/eval_jaxpr/ppermute | solution.py:275
  162.3 7.6 %collective-permute-done.2 = bf16[10,128,256]{2,1,0:T(8,128)(2,1)} collective-permute-done((bf16[10,128,256]{2,1,0:T(8,128)(2,1)S(1)}, bf16[10,128,256]{2,1,0:T(8,128)(2,1)}, u32[]{:S(2)}, u32[]{:S(2)}) %collective-permute-start.2) | collective-permute-done | bytes 655392 | tf_op jit(solution)/shard_map/while/body/eval_jaxpr/ppermute | solution.py:275
  169.9 12.0 %forward.8 = (bf16[10,128,256]{2,1,0:T(8,128)(2,1)S(1)}, bf16[4,28,128,256]{3,2,1,0:T(8,128)(2,1)}, bf16[4,4,128,256]{3,2,1,0:T(8,128)(2,1)}, bf16[4,6,128,256]{...) custom-call(s32[8]{0:T(128)S(1)} %stack.268.flags, ...), custom_call_target="tpu_custom_call", output_to_operand_aliasing={{1}: (14, {}), {2}: (15, {}), {3}: (16, {}), {4}: (17, {})} | custom-call | tf_op jit(solution)/shard_map/while/body/eval_jaxpr/forward/pallas_call | solution.py:435
  181.9 5.3 %collective-permute-start.2 = (bf16[10,128,256]{2,1,0:T(8,128)(2,1)S(1)}, bf16[10,128,256]{2,1,0:T(8,128)(2,1)}, u32[]{:S(2)}, u32[]{:S(2)}) collective-permute-start(bf16[10,128,256]{2,1,0:T(8,128)(2,1)S(1)} %get-tuple-element.1618), channel_id=1, source_target_pairs={{16,32},{32,16},{48,64},{64,48},{80,96},{96,80},{112,128},{128,112... | collective-permute-start | bytes 1966088 | tf_op jit(solution)/shard_map/while/body/eval_jaxpr/ppermute | solution.py:275
  188.2 7.9 %collective-permute-done.2 = bf16[10,128,256]{2,1,0:T(8,128)(2,1)} collective-permute-done((bf16[10,128,256]{2,1,0:T(8,128)(2,1)S(1)}, bf16[10,128,256]{2,1,0:T(8,128)(2,1)}, u32[]{:S(2)}, u32[]{:S(2)}) %collective-permute-start.2) | collective-permute-done | bytes 655392 | tf_op jit(solution)/shard_map/while/body/eval_jaxpr/ppermute | solution.py:275
  196.1 12.0 %forward.8 = (bf16[10,128,256]{2,1,0:T(8,128)(2,1)S(1)}, bf16[4,28,128,256]{3,2,1,0:T(8,128)(2,1)}, bf16[4,4,128,256]{3,2,1,0:T(8,128)(2,1)}, bf16[4,6,128,256]{...) custom-call(s32[8]{0:T(128)S(1)} %stack.268.flags, ...), custom_call_target="tpu_custom_call", output_to_operand_aliasing={{1}: (14, {}), {2}: (15, {}), {3}: (16, {}), {4}: (17, {})} | custom-call | tf_op jit(solution)/shard_map/while/body/eval_jaxpr/forward/pallas_call | solution.py:435
  208.1 5.0 %collective-permute-start.2 = (bf16[10,128,256]{2,1,0:T(8,128)(2,1)S(1)}, bf16[10,128,256]{2,1,0:T(8,128)(2,1)}, u32[]{:S(2)}, u32[]{:S(2)}) collective-permute-start(bf16[10,128,256]{2,1,0:T(8,128)(2,1)S(1)} %get-tuple-element.1618), channel_id=1, source_target_pairs={{16,32},{32,16},{48,64},{64,48},{80,96},{96,80},{112,128},{128,112... | collective-permute-start | bytes 1966088 | tf_op jit(solution)/shard_map/while/body/eval_jaxpr/ppermute | solution.py:275
  214.2 8.1 %collective-permute-done.2 = bf16[10,128,256]{2,1,0:T(8,128)(2,1)} collective-permute-done((bf16[10,128,256]{2,1,0:T(8,128)(2,1)S(1)}, bf16[10,128,256]{2,1,0:T(8,128)(2,1)}, u32[]{:S(2)}, u32[]{:S(2)}) %collective-permute-start.2) | collective-permute-done | bytes 655392 | tf_op jit(solution)/shard_map/while/body/eval_jaxpr/ppermute | solution.py:275
  222.2 79.0 %while.49 = (s32[]{:T(128)}, bf16[4,128,256]{2,1,0:T(8,128)(2,1)}, bf16[4,128,256]{2,1,0:T(8,128)(2,1)}, bf16[4,128,256]{2,1,0:T(8,128)(2,1)}, bf16[4,4,128,256]...) while((s32[]{:T(128)}, bf16[4,128,256]{2,1,0:T(8,128)(2,1)}, ...), condition=%wide.region_5.6_spmd, body=%wide.region_2.5_spmd.sunk | while | flops 23 | bytes 2622094 | solution.py:491
  222.3 11.3 %backward.8 = (bf16[4,128,256]{2,1,0:T(8,128)(2,1)S(1)}, bf16[4,4,128,256]{3,2,1,0:T(8,128)(2,1)}) custom-call(s32[8]{0:T(128)S(1)} %stack.271.flags, bf16[4,128,256]{2,1,0:T(8,128)(2,1)} %get-tuple-element.1678.own, bf16[4,128,256]{2,1,0:T(8,128)(2,1)} %get-tuple-element.1679.outside, ...), custom_call_target="tpu_custom_call", output_to_operand_aliasing={{1}: (19, {})} | custom-call | tf_op jit(solution)/shard_map/while/body/eval_jaxpr/backward/pallas_call | solution.py:483
  233.7 9.9 %conditional.2 = ((bf16[4,128,256]{2,1,0:T(8,128)(2,1)}, bf16[4,128,256]{2,1,0:T(8,128)(2,1)})) conditional(s32[]{:T(128)} %convert_element_type.44, (bf16[4,128,256]{2,1,0:T(8,128)(2,1)}, bf16[4,128,256]{2,1,0:T(8,128)(2,1)}) %tuple.95, bf16[4,128,256]{2,1,0:T(8,128)(2,1)S(1)} %get-tuple-element.1709), branch_computations={%region_3.3_spmd, %region_4.4_spmd} | conditional | bytes 2097256 | solution.py:487
  233.7 4.9 %collective-permute-start = (bf16[4,128,256]{2,1,0:T(8,128)(2,1)S(1)}, bf16[4,128,256]{2,1,0:T(8,128)(2,1)}, u32[]{:S(2)}, u32[]{:S(2)}) collective-permute-start(bf16[4,128,256]{2,1,0:T(8,128)(2,1)S(1)} %param.3), channel_id=1, source_target_pairs={{16,32},{32,16},{48,64},{64,48},{80,96},{96,80},{112,128},{128,112... | collective-permute-start | bytes 786440 | tf_op jit(solution)/shard_map/while/body/eval_jaxpr/cond/branch_1_fun/ppermute | solution.py:275
  238.7 4.9 %collective-permute-done = bf16[4,128,256]{2,1,0:T(8,128)(2,1)} collective-permute-done((bf16[4,128,256]{2,1,0:T(8,128)(2,1)S(1)}, bf16[4,128,256]{2,1,0:T(8,128)(2,1)}, u32[]{:S(2)}, u32[]{:S(2)}) %collective-permute-start) | collective-permute-done | bytes 262176 | tf_op jit(solution)/shard_map/while/body/eval_jaxpr/cond/branch_1_fun/ppermute | solution.py:275
  244.4 11.2 %backward.8 = (bf16[4,128,256]{2,1,0:T(8,128)(2,1)S(1)}, bf16[4,4,128,256]{3,2,1,0:T(8,128)(2,1)}) custom-call(s32[8]{0:T(128)S(1)} %stack.271.flags, bf16[4,128,256]{2,1,0:T(8,128)(2,1)} %get-tuple-element.1678.own, bf16[4,128,256]{2,1,0:T(8,128)(2,1)} %get-tuple-element.1679.outside, ...), custom_call_target="tpu_custom_call", output_to_operand_aliasing={{1}: (19, {})} | custom-call | tf_op jit(solution)/shard_map/while/body/eval_jaxpr/backward/pallas_call | solution.py:483
  255.6 9.9 %conditional.2 = ((bf16[4,128,256]{2,1,0:T(8,128)(2,1)}, bf16[4,128,256]{2,1,0:T(8,128)(2,1)})) conditional(s32[]{:T(128)} %convert_element_type.44, (bf16[4,128,256]{2,1,0:T(8,128)(2,1)}, bf16[4,128,256]{2,1,0:T(8,128)(2,1)}) %tuple.95, bf16[4,128,256]{2,1,0:T(8,128)(2,1)S(1)} %get-tuple-element.1709), branch_computations={%region_3.3_spmd, %region_4.4_spmd} | conditional | bytes 2097256 | solution.py:487
  255.6 5.0 %collective-permute-start = (bf16[4,128,256]{2,1,0:T(8,128)(2,1)S(1)}, bf16[4,128,256]{2,1,0:T(8,128)(2,1)}, u32[]{:S(2)}, u32[]{:S(2)}) collective-permute-start(bf16[4,128,256]{2,1,0:T(8,128)(2,1)S(1)} %param.3), channel_id=1, source_target_pairs={{16,32},{32,16},{48,64},{64,48},{80,96},{96,80},{112,128},{128,112... | collective-permute-start | bytes 786440 | tf_op jit(solution)/shard_map/while/body/eval_jaxpr/cond/branch_1_fun/ppermute | solution.py:275
  260.7 4.8 %collective-permute-done = bf16[4,128,256]{2,1,0:T(8,128)(2,1)} collective-permute-done((bf16[4,128,256]{2,1,0:T(8,128)(2,1)S(1)}, bf16[4,128,256]{2,1,0:T(8,128)(2,1)}, u32[]{:S(2)}, u32[]{:S(2)}) %collective-permute-start) | collective-permute-done | bytes 262176 | tf_op jit(solution)/shard_map/while/body/eval_jaxpr/cond/branch_1_fun/ppermute | solution.py:275
  266.3 11.2 %backward.8 = (bf16[4,128,256]{2,1,0:T(8,128)(2,1)S(1)}, bf16[4,4,128,256]{3,2,1,0:T(8,128)(2,1)}) custom-call(s32[8]{0:T(128)S(1)} %stack.271.flags, bf16[4,128,256]{2,1,0:T(8,128)(2,1)} %get-tuple-element.1678.own, bf16[4,128,256]{2,1,0:T(8,128)(2,1)} %get-tuple-element.1679.outside, ...), custom_call_target="tpu_custom_call", output_to_operand_aliasing={{1}: (19, {})} | custom-call | tf_op jit(solution)/shard_map/while/body/eval_jaxpr/backward/pallas_call | solution.py:483
  277.6 9.9 %conditional.2 = ((bf16[4,128,256]{2,1,0:T(8,128)(2,1)}, bf16[4,128,256]{2,1,0:T(8,128)(2,1)})) conditional(s32[]{:T(128)} %convert_element_type.44, (bf16[4,128,256]{2,1,0:T(8,128)(2,1)}, bf16[4,128,256]{2,1,0:T(8,128)(2,1)}) %tuple.95, bf16[4,128,256]{2,1,0:T(8,128)(2,1)S(1)} %get-tuple-element.1709), branch_computations={%region_3.3_spmd, %region_4.4_spmd} | conditional | bytes 2097256 | solution.py:487
  277.6 5.1 %collective-permute-start = (bf16[4,128,256]{2,1,0:T(8,128)(2,1)S(1)}, bf16[4,128,256]{2,1,0:T(8,128)(2,1)}, u32[]{:S(2)}, u32[]{:S(2)}) collective-permute-start(bf16[4,128,256]{2,1,0:T(8,128)(2,1)S(1)} %param.3), channel_id=1, source_target_pairs={{16,32},{32,16},{48,64},{64,48},{80,96},{96,80},{112,128},{128,112... | collective-permute-start | bytes 786440 | tf_op jit(solution)/shard_map/while/body/eval_jaxpr/cond/branch_1_fun/ppermute | solution.py:275
  282.8 4.7 %collective-permute-done = bf16[4,128,256]{2,1,0:T(8,128)(2,1)} collective-permute-done((bf16[4,128,256]{2,1,0:T(8,128)(2,1)S(1)}, bf16[4,128,256]{2,1,0:T(8,128)(2,1)}, u32[]{:S(2)}, u32[]{:S(2)}) %collective-permute-start) | collective-permute-done | bytes 262176 | tf_op jit(solution)/shard_map/while/body/eval_jaxpr/cond/branch_1_fun/ppermute | solution.py:275
  288.3 12.2 %backward.8 = (bf16[4,128,256]{2,1,0:T(8,128)(2,1)S(1)}, bf16[4,4,128,256]{3,2,1,0:T(8,128)(2,1)}) custom-call(s32[8]{0:T(128)S(1)} %stack.271.flags, bf16[4,128,256]{2,1,0:T(8,128)(2,1)} %get-tuple-element.1678.own, bf16[4,128,256]{2,1,0:T(8,128)(2,1)} %get-tuple-element.1679.outside, ...), custom_call_target="tpu_custom_call", output_to_operand_aliasing={{1}: (19, {})} | custom-call | tf_op jit(solution)/shard_map/while/body/eval_jaxpr/backward/pallas_call | solution.py:483
  301.2 2.1 dynamic-slice_bitcast_fusion
  303.9 4.2 %collective-permute-start.27 = (bf16[4,128,256]{2,1,0:T(8,128)(2,1)S(1)}, bf16[4,128,256]{2,1,0:T(8,128)(2,1)S(1)}, u32[]{:S(2)}, u32[]{:S(2)}) collective-permute-start(bf16[4,128,256]{2,1,0:T(8,128)(2,1)S(1)} %get-tuple-element.1223), channel_id=1, source_target_pairs={{0,2},{1,3},{2,0},{3,1},{4,6},{5,7},{6,4},{7,5},{8,10},{9,11},{10,... | collective-permute-start | bytes 786440 | tf_op jit(solution)/shard_map/ppermute | solution.py:275
  312.1 3.2 collective-permute-start.25
  316.0 4.3 %collective-permute-done.27.refs_2_ = bf16[4,128,256]{2,1,0:T(8,128)(2,1)S(1)} collective-permute-done((bf16[4,128,256]{2,1,0:T(8,128)(2,1)S(1)}, bf16[4,128,256]{2,1,0:T(8,128)(2,1)S(1)}, u32[]{:S(2)}, u32[]{:S(2)}) %collective-permute-start.27) | collective-permute-done | bytes 262176 | tf_op jit(solution)/shard_map/ppermute | solution.py:275
  321.0 2.2 set_in_order.3
  323.2 6.2 %collective-permute-done.24.refs_2_ = bf16[4,128,256]{2,1,0:T(8,128)(2,1)S(1)} collective-permute-done((bf16[4,128,256]{2,1,0:T(8,128)(2,1)}, bf16[4,128,256]{2,1,0:T(8,128)(2,1)S(1)}, u32[]{:S(2)}, u32[]{:S(2)}) %collective-permute-start.24) | collective-permute-done | bytes 262176 | tf_op jit(solution)/shard_map/ppermute | solution.py:275
  330.2 2.2 set_in_order.2
  (108 shorter events, 32.0 us)
Async XLA Ops:
  0.6 6.2 %copy-start = (bf16[1,3,3,256,256]{4,3,2,1,0:T(8,128)(2,1)S(1)}, bf16[1,3,3,256,256]{4,3,2,1,0:T(8,128)(2,1)}, u32[]{:S(2)}) copy-start(bf16[1,3,3,256,256]{4,3,2,1,0:T(8,128)(2,1)} %param.12) | copy-start | bytes 3538948
  0.6 6.2 %copy-start.10 = (f32[1,256]{1,0:T(1,128)S(1)}, f32[1,256]{1,0:T(1,128)}, u32[]{:S(2)}) copy-start(f32[1,256]{1,0:T(1,128)} %param.13) | copy-start | bytes 3076
  2.8 34.5 %copy-start.3 = (bf16[4,128,256]{2,1,0:T(8,128)(2,1)}, bf16[4,128,256]{2,1,0:T(8,128)(2,1)S(1)}, u32[]{:S(2)}) copy-start(bf16[4,128,256]{2,1,0:T(8,128)(2,1)S(1)} %get-tuple-element.1647) | copy-start | bytes 786436
  2.9 43.8 %copy-start.2 = (bf16[10,128,256]{2,1,0:T(8,128)(2,1)}, bf16[10,128,256]{2,1,0:T(8,128)(2,1)S(1)}, u32[]{:S(2)}) copy-start(bf16[10,128,256]{2,1,0:T(8,128)(2,1)S(1)} %pad_maximum_fusion.1) | copy-start | bytes 1966084
  2.9 32.3 %collective-permute-start.4 = (bf16[10,128,256]{2,1,0:T(8,128)(2,1)S(1)}, bf16[10,128,256]{2,1,0:T(8,128)(2,1)}, u32[]{:S(2)}, u32[]{:S(2)}) collective-permute-start(bf16[10,128,256]{2,1,0:T(8,128)(2,1)S(1)} %pad_maximum_fusion.1), channel_id=1, source_target_pairs={{16,32},{32,16},{48,64},{64,48},{80,96},{96,80},{112,128},{128,112... | collective-permute-start | bytes 1966088 | tf_op jit(solution)/shard_map/ppermute | solution.py:275
  6.6 28.5 %collective-permute-start.5 = (bf16[10,128,256]{2,1,0:T(8,128)(2,1)S(1)}, bf16[10,128,256]{2,1,0:T(8,128)(2,1)}, u32[]{:S(2)}, u32[]{:S(2)}) collective-permute-start(bf16[10,128,256]{2,1,0:T(8,128)(2,1)S(1)} %pad_maximum_fusion.1), channel_id=1, source_target_pairs={{0,16},{16,0},{32,48},{48,32},{64,80},{80,64},{96,112},{112,96},{1... | collective-permute-start | bytes 1966088 | tf_op jit(solution)/shard_map/ppermute | solution.py:275
  7.0 21.9 %collective-permute-start.6 = (bf16[304,256]{1,0:T(8,128)(2,1)S(1)}, bf16[304,256]{1,0:T(8,128)(2,1)S(1)}, u32[]{:S(2)}, u32[]{:S(2)}) collective-permute-start(bf16[304,256]{1,0:T(8,128)(2,1)S(1)} %concatenate.14), channel_id=1, source_target_pairs={{0,4},{1,5},{2,6},{3,7},{4,8},{5,9},{6,10},{7,11},{8,12},{9,13},{1... | collective-permute-start | bytes 466952 | tf_op jit(solution)/shard_map/ppermute | solution.py:306
  10.1 18.8 %collective-permute-start.7 = (bf16[304,256]{1,0:T(8,128)(2,1)S(1)}, bf16[304,256]{1,0:T(8,128)(2,1)S(1)}, u32[]{:S(2)}, u32[]{:S(2)}) collective-permute-start(bf16[304,256]{1,0:T(8,128)(2,1)S(1)} %concatenate.14), channel_id=1, source_target_pairs={{0,12},{1,13},{2,14},{3,15},{4,0},{5,1},{6,2},{7,3},{8,4},{9,5},{1... | collective-permute-start | bytes 466952 | tf_op jit(solution)/shard_map/ppermute | solution.py:306
  28.9 5.4 %collective-permute-start.8 = (bf16[152,256]{1,0:T(8,128)(2,1)S(1)}, bf16[152,256]{1,0:T(8,128)(2,1)S(1)}, u32[]{:S(2)}, u32[]{:S(2)}) collective-permute-start(bf16[152,256]{1,0:T(8,128)(2,1)S(1)} %slice.32), channel_id=1, source_target_pairs={{0,4},{1,5},{2,6},{3,7},{4,8},{5,9},{6,10},{7,11},{8,12},{9,13},{1... | collective-permute-start | bytes 233480 | tf_op jit(solution)/shard_map/ppermute | solution.py:306
  28.9 5.3 %collective-permute-start.9 = (bf16[152,256]{1,0:T(8,128)(2,1)S(1)}, bf16[152,256]{1,0:T(8,128)(2,1)S(1)}, u32[]{:S(2)}, u32[]{:S(2)}) collective-permute-start(bf16[152,256]{1,0:T(8,128)(2,1)S(1)} %slice.33), channel_id=1, source_target_pairs={{0,12},{1,13},{2,14},{3,15},{4,0},{5,1},{6,2},{7,3},{8,4},{9,5},{1... | collective-permute-start | bytes 233480 | tf_op jit(solution)/shard_map/ppermute | solution.py:306
  37.3 18.0 %copy-start.4 = (bf16[4,304,256]{2,1,0:T(8,128)(2,1)S(1)}, bf16[4,304,256]{2,1,0:T(8,128)(2,1)}, u32[]{:S(2)}) copy-start(bf16[4,304,256]{2,1,0:T(8,128)(2,1)} %get-tuple-element.1111) | copy-start | bytes 1867780
  37.3 9.3 %collective-permute-start.10 = (bf16[4,304,256]{2,1,0:T(8,128)(2,1)}, bf16[4,304,256]{2,1,0:T(8,128)(2,1)S(1)}, u32[]{:S(2)}, u32[]{:S(2)}) collective-permute-start(bf16[4,304,256]{2,1,0:T(8,128)(2,1)} %get-tuple-element.1111), channel_id=1, source_target_pairs={{0,1},{1,2},{2,3},{3,0},{4,5},{5,6},{6,7},{7,4},{8,9},{9,10},{10,1... | collective-permute-start | bytes 1867784 | tf_op jit(solution)/shard_map/ppermute | solution.py:306
  37.3 10.9 %collective-permute-start.11 = (bf16[4,304,256]{2,1,0:T(8,128)(2,1)}, bf16[4,304,256]{2,1,0:T(8,128)(2,1)S(1)}, u32[]{:S(2)}, u32[]{:S(2)}) collective-permute-start(bf16[4,304,256]{2,1,0:T(8,128)(2,1)} %get-tuple-element.1111), channel_id=1, source_target_pairs={{0,3},{1,0},{2,1},{3,2},{4,7},{5,4},{6,5},{7,6},{8,11},{9,8},{10,9... | collective-permute-start | bytes 1867784 | tf_op jit(solution)/shard_map/ppermute | solution.py:306
  46.6 5.8 %collective-permute-start.12 = (bf16[2,304,256]{2,1,0:T(8,128)(2,1)S(1)}, bf16[2,304,256]{2,1,0:T(8,128)(2,1)S(1)}, u32[]{:S(2)}, u32[]{:S(2)}) collective-permute-start(bf16[2,304,256]{2,1,0:T(8,128)(2,1)S(1)} %slice.34), channel_id=1, source_target_pairs={{0,1},{1,2},{2,3},{3,0},{4,5},{5,6},{6,7},{7,4},{8,9},{9,10},{10,1... | collective-permute-start | bytes 933896 | tf_op jit(solution)/shard_map/ppermute | solution.py:306
  48.2 7.0 %collective-permute-start.13 = (bf16[2,304,256]{2,1,0:T(8,128)(2,1)S(1)}, bf16[2,304,256]{2,1,0:T(8,128)(2,1)S(1)}, u32[]{:S(2)}, u32[]{:S(2)}) collective-permute-start(bf16[2,304,256]{2,1,0:T(8,128)(2,1)S(1)} %slice.35), channel_id=1, source_target_pairs={{0,3},{1,0},{2,1},{3,2},{4,7},{5,4},{6,5},{7,6},{8,11},{9,8},{10,9... | collective-permute-start | bytes 933896 | tf_op jit(solution)/shard_map/ppermute | solution.py:306
  57.1 30.6 %collective-permute-start.14 = (bf16[4,4,304,256]{3,2,1,0:T(8,128)(2,1)}, bf16[4,4,304,256]{3,2,1,0:T(8,128)(2,1)}, u32[]{:S(2)}, u32[]{:S(2)}) collective-permute-start(bf16[4,4,304,256]{3,2,1,0:T(8,128)(2,1)} %pad_maximum_fusion), channel_id=1, source_target_pairs={{0,32},{1,33},{2,34},{3,35},{4,36},{5,37},{6,38},{7,39},{8,40},{9,... | collective-permute-start | bytes 7471112 | tf_op jit(solution)/shard_map/ppermute | solution.py:306
  58.2 31.1 %collective-permute-start.15 = (bf16[4,4,304,256]{3,2,1,0:T(8,128)(2,1)}, bf16[4,4,304,256]{3,2,1,0:T(8,128)(2,1)}, u32[]{:S(2)}, u32[]{:S(2)}) collective-permute-start(bf16[4,4,304,256]{3,2,1,0:T(8,128)(2,1)} %pad_maximum_fusion), channel_id=1, source_target_pairs={{0,96},{1,97},{2,98},{3,99},{4,100},{5,101},{6,102},{7,103},{8,104... | collective-permute-start | bytes 7471112 | tf_op jit(solution)/shard_map/ppermute | solution.py:306
  59.8 47.9 %collective-permute-start.18 = (bf16[4,4,304,256]{3,2,1,0:T(8,128)(2,1)}, bf16[4,4,304,256]{3,2,1,0:T(8,128)(2,1)}, u32[]{:S(2)}, u32[]{:S(2)}) collective-permute-start(bf16[4,4,304,256]{3,2,1,0:T(8,128)(2,1)} %pad_maximum_fusion), channel_id=1, source_target_pairs={{0,16},{1,17},{2,18},{3,19},{4,20},{5,21},{6,22},{7,23},{8,24},{9,... | collective-permute-start | bytes 7471112 | tf_op jit(solution)/shard_map/ppermute | solution.py:306
  89.1 17.4 %collective-permute-start.16 = (bf16[2,4,304,256]{3,2,1,0:T(8,128)(2,1)S(1)}, bf16[2,4,304,256]{3,2,1,0:T(8,128)(2,1)}, u32[]{:S(2)}, u32[]{:S(2)}) collective-permute-start(bf16[2,4,304,256]{3,2,1,0:T(8,128)(2,1)S(1)} %slice.36), channel_id=1, source_target_pairs={{0,32},{1,33},{2,34},{3,35},{4,36},{5,37},{6,38},{7,39},{8,40},{9,... | collective-permute-start | bytes 3735560 | tf_op jit(solution)/shard_map/ppermute | solution.py:306
  90.6 16.6 %collective-permute-start.17 = (bf16[2,4,304,256]{3,2,1,0:T(8,128)(2,1)S(1)}, bf16[2,4,304,256]{3,2,1,0:T(8,128)(2,1)}, u32[]{:S(2)}, u32[]{:S(2)}) collective-permute-start(bf16[2,4,304,256]{3,2,1,0:T(8,128)(2,1)S(1)} %slice.37), channel_id=1, source_target_pairs={{0,96},{1,97},{2,98},{3,99},{4,100},{5,101},{6,102},{7,103},{8,104... | collective-permute-start | bytes 3735560 | tf_op jit(solution)/shard_map/ppermute | solution.py:306
  93.4 18.3 %collective-permute-start.19 = (bf16[4,4,304,256]{3,2,1,0:T(8,128)(2,1)}, bf16[4,4,304,256]{3,2,1,0:T(8,128)(2,1)}, u32[]{:S(2)}, u32[]{:S(2)}) collective-permute-start(bf16[4,4,304,256]{3,2,1,0:T(8,128)(2,1)} %collective-permute-done.14), channel_id=1, source_target_pairs={{0,16},{1,17},{2,18},{3,19},{4,20},{5,21},{6,22},{7,23},{8,24},{9,... | collective-permute-start | bytes 7471112 | tf_op jit(solution)/shard_map/ppermute | solution.py:306
  93.4 18.3 %collective-permute-start.20 = (bf16[4,4,304,256]{3,2,1,0:T(8,128)(2,1)}, bf16[4,4,304,256]{3,2,1,0:T(8,128)(2,1)}, u32[]{:S(2)}, u32[]{:S(2)}) collective-permute-start(bf16[4,4,304,256]{3,2,1,0:T(8,128)(2,1)} %collective-permute-done.15), channel_id=1, source_target_pairs={{0,16},{1,17},{2,18},{3,19},{4,20},{5,21},{6,22},{7,23},{8,24},{9,... | collective-permute-start | bytes 7471112 | tf_op jit(solution)/shard_map/ppermute | solution.py:306
  106.6 3.3 collective-permute-start.21
  107.2 4.4 %collective-permute-start.22 = (bf16[2,4,304,256]{3,2,1,0:T(8,128)(2,1)}, bf16[2,4,304,256]{3,2,1,0:T(8,128)(2,1)}, u32[]{:S(2)}, u32[]{:S(2)}) collective-permute-start(bf16[2,4,304,256]{3,2,1,0:T(8,128)(2,1)} %collective-permute-done.17), channel_id=1, source_target_pairs={{0,16},{1,17},{2,18},{3,19},{4,20},{5,21},{6,22},{7,23},{8,24},{9,... | collective-permute-start | bytes 3735560 | tf_op jit(solution)/shard_map/ppermute | solution.py:306
  124.1 19.6 %collective-permute-start.2 = (bf16[10,128,256]{2,1,0:T(8,128)(2,1)S(1)}, bf16[10,128,256]{2,1,0:T(8,128)(2,1)}, u32[]{:S(2)}, u32[]{:S(2)}) collective-permute-start(bf16[10,128,256]{2,1,0:T(8,128)(2,1)S(1)} %get-tuple-element.1618), channel_id=1, source_target_pairs={{16,32},{32,16},{48,64},{64,48},{80,96},{96,80},{112,128},{128,112... | collective-permute-start | bytes 1966088 | tf_op jit(solution)/shard_map/while/body/eval_jaxpr/ppermute | solution.py:275
  135.3 8.4 %collective-permute-start.3 = (bf16[10,128,256]{2,1,0:T(8,128)(2,1)S(1)}, bf16[10,128,256]{2,1,0:T(8,128)(2,1)}, u32[]{:S(2)}, u32[]{:S(2)}) collective-permute-start(bf16[10,128,256]{2,1,0:T(8,128)(2,1)S(1)} %get-tuple-element.1618), channel_id=1, source_target_pairs={{0,16},{16,0},{32,48},{48,32},{64,80},{80,64},{96,112},{112,96},{1... | collective-permute-start | bytes 1966088 | tf_op jit(solution)/shard_map/while/body/eval_jaxpr/ppermute | solution.py:275
  155.7 14.1 %collective-permute-start.2 = (bf16[10,128,256]{2,1,0:T(8,128)(2,1)S(1)}, bf16[10,128,256]{2,1,0:T(8,128)(2,1)}, u32[]{:S(2)}, u32[]{:S(2)}) collective-permute-start(bf16[10,128,256]{2,1,0:T(8,128)(2,1)S(1)} %get-tuple-element.1618), channel_id=1, source_target_pairs={{16,32},{32,16},{48,64},{64,48},{80,96},{96,80},{112,128},{128,112... | collective-permute-start | bytes 1966088 | tf_op jit(solution)/shard_map/while/body/eval_jaxpr/ppermute | solution.py:275
  161.3 8.6 %collective-permute-start.3 = (bf16[10,128,256]{2,1,0:T(8,128)(2,1)S(1)}, bf16[10,128,256]{2,1,0:T(8,128)(2,1)}, u32[]{:S(2)}, u32[]{:S(2)}) collective-permute-start(bf16[10,128,256]{2,1,0:T(8,128)(2,1)S(1)} %get-tuple-element.1618), channel_id=1, source_target_pairs={{0,16},{16,0},{32,48},{48,32},{64,80},{80,64},{96,112},{112,96},{1... | collective-permute-start | bytes 1966088 | tf_op jit(solution)/shard_map/while/body/eval_jaxpr/ppermute | solution.py:275
  181.9 14.1 %collective-permute-start.2 = (bf16[10,128,256]{2,1,0:T(8,128)(2,1)S(1)}, bf16[10,128,256]{2,1,0:T(8,128)(2,1)}, u32[]{:S(2)}, u32[]{:S(2)}) collective-permute-start(bf16[10,128,256]{2,1,0:T(8,128)(2,1)S(1)} %get-tuple-element.1618), channel_id=1, source_target_pairs={{16,32},{32,16},{48,64},{64,48},{80,96},{96,80},{112,128},{128,112... | collective-permute-start | bytes 1966088 | tf_op jit(solution)/shard_map/while/body/eval_jaxpr/ppermute | solution.py:275
  187.2 8.9 %collective-permute-start.3 = (bf16[10,128,256]{2,1,0:T(8,128)(2,1)S(1)}, bf16[10,128,256]{2,1,0:T(8,128)(2,1)}, u32[]{:S(2)}, u32[]{:S(2)}) collective-permute-start(bf16[10,128,256]{2,1,0:T(8,128)(2,1)S(1)} %get-tuple-element.1618), channel_id=1, source_target_pairs={{0,16},{16,0},{32,48},{48,32},{64,80},{80,64},{96,112},{112,96},{1... | collective-permute-start | bytes 1966088 | tf_op jit(solution)/shard_map/while/body/eval_jaxpr/ppermute | solution.py:275
  208.1 14.1 %collective-permute-start.2 = (bf16[10,128,256]{2,1,0:T(8,128)(2,1)S(1)}, bf16[10,128,256]{2,1,0:T(8,128)(2,1)}, u32[]{:S(2)}, u32[]{:S(2)}) collective-permute-start(bf16[10,128,256]{2,1,0:T(8,128)(2,1)S(1)} %get-tuple-element.1618), channel_id=1, source_target_pairs={{16,32},{32,16},{48,64},{64,48},{80,96},{96,80},{112,128},{128,112... | collective-permute-start | bytes 1966088 | tf_op jit(solution)/shard_map/while/body/eval_jaxpr/ppermute | solution.py:275
  213.2 9.1 %collective-permute-start.3 = (bf16[10,128,256]{2,1,0:T(8,128)(2,1)S(1)}, bf16[10,128,256]{2,1,0:T(8,128)(2,1)}, u32[]{:S(2)}, u32[]{:S(2)}) collective-permute-start(bf16[10,128,256]{2,1,0:T(8,128)(2,1)S(1)} %get-tuple-element.1618), channel_id=1, source_target_pairs={{0,16},{16,0},{32,48},{48,32},{64,80},{80,64},{96,112},{112,96},{1... | collective-permute-start | bytes 1966088 | tf_op jit(solution)/shard_map/while/body/eval_jaxpr/ppermute | solution.py:275
  233.7 9.9 %collective-permute-start = (bf16[4,128,256]{2,1,0:T(8,128)(2,1)S(1)}, bf16[4,128,256]{2,1,0:T(8,128)(2,1)}, u32[]{:S(2)}, u32[]{:S(2)}) collective-permute-start(bf16[4,128,256]{2,1,0:T(8,128)(2,1)S(1)} %param.3), channel_id=1, source_target_pairs={{16,32},{32,16},{48,64},{64,48},{80,96},{96,80},{112,128},{128,112... | collective-permute-start | bytes 786440 | tf_op jit(solution)/shard_map/while/body/eval_jaxpr/cond/branch_1_fun/ppermute | solution.py:275
  238.6 5.0 %collective-permute-start.1 = (bf16[4,128,256]{2,1,0:T(8,128)(2,1)S(1)}, bf16[4,128,256]{2,1,0:T(8,128)(2,1)}, u32[]{:S(2)}, u32[]{:S(2)}) collective-permute-start(bf16[4,128,256]{2,1,0:T(8,128)(2,1)S(1)} %param.3), channel_id=1, source_target_pairs={{0,16},{16,0},{32,48},{48,32},{64,80},{80,64},{96,112},{112,96},{1... | collective-permute-start | bytes 786440 | tf_op jit(solution)/shard_map/while/body/eval_jaxpr/cond/branch_1_fun/ppermute | solution.py:275
  255.6 9.9 %collective-permute-start = (bf16[4,128,256]{2,1,0:T(8,128)(2,1)S(1)}, bf16[4,128,256]{2,1,0:T(8,128)(2,1)}, u32[]{:S(2)}, u32[]{:S(2)}) collective-permute-start(bf16[4,128,256]{2,1,0:T(8,128)(2,1)S(1)} %param.3), channel_id=1, source_target_pairs={{16,32},{32,16},{48,64},{64,48},{80,96},{96,80},{112,128},{128,112... | collective-permute-start | bytes 786440 | tf_op jit(solution)/shard_map/while/body/eval_jaxpr/cond/branch_1_fun/ppermute | solution.py:275
  260.6 4.9 %collective-permute-start.1 = (bf16[4,128,256]{2,1,0:T(8,128)(2,1)S(1)}, bf16[4,128,256]{2,1,0:T(8,128)(2,1)}, u32[]{:S(2)}, u32[]{:S(2)}) collective-permute-start(bf16[4,128,256]{2,1,0:T(8,128)(2,1)S(1)} %param.3), channel_id=1, source_target_pairs={{0,16},{16,0},{32,48},{48,32},{64,80},{80,64},{96,112},{112,96},{1... | collective-permute-start | bytes 786440 | tf_op jit(solution)/shard_map/while/body/eval_jaxpr/cond/branch_1_fun/ppermute | solution.py:275
  277.6 9.9 %collective-permute-start = (bf16[4,128,256]{2,1,0:T(8,128)(2,1)S(1)}, bf16[4,128,256]{2,1,0:T(8,128)(2,1)}, u32[]{:S(2)}, u32[]{:S(2)}) collective-permute-start(bf16[4,128,256]{2,1,0:T(8,128)(2,1)S(1)} %param.3), channel_id=1, source_target_pairs={{16,32},{32,16},{48,64},{64,48},{80,96},{96,80},{112,128},{128,112... | collective-permute-start | bytes 786440 | tf_op jit(solution)/shard_map/while/body/eval_jaxpr/cond/branch_1_fun/ppermute | solution.py:275
  282.7 4.8 %collective-permute-start.1 = (bf16[4,128,256]{2,1,0:T(8,128)(2,1)S(1)}, bf16[4,128,256]{2,1,0:T(8,128)(2,1)}, u32[]{:S(2)}, u32[]{:S(2)}) collective-permute-start(bf16[4,128,256]{2,1,0:T(8,128)(2,1)S(1)} %param.3), channel_id=1, source_target_pairs={{0,16},{16,0},{32,48},{48,32},{64,80},{80,64},{96,112},{112,96},{1... | collective-permute-start | bytes 786440 | tf_op jit(solution)/shard_map/while/body/eval_jaxpr/cond/branch_1_fun/ppermute | solution.py:275
  301.2 6.8 %copy-start.1 = (bf16[4,4,128,256]{3,2,1,0:T(8,128)(2,1)S(1)}, bf16[4,4,128,256]{3,2,1,0:T(8,128)(2,1)}, u32[]{:S(2)}) copy-start(bf16[4,4,128,256]{3,2,1,0:T(8,128)(2,1)} %get-tuple-element.1112) | copy-start | bytes 3145732
  303.3 8.8 %collective-permute-start.26 = (bf16[4,128,256]{2,1,0:T(8,128)(2,1)S(1)}, bf16[4,128,256]{2,1,0:T(8,128)(2,1)S(1)}, u32[]{:S(2)}, u32[]{:S(2)}) collective-permute-start(bf16[4,128,256]{2,1,0:T(8,128)(2,1)S(1)} %get-tuple-element.1224), channel_id=1, source_target_pairs={{0,1},{1,2},{2,3},{3,0},{4,5},{5,6},{6,7},{7,4},{8,9},{9,10},{10,1... | collective-permute-start | bytes 786440 | tf_op jit(solution)/shard_map/ppermute | solution.py:275
  303.9 16.4 %collective-permute-start.27 = (bf16[4,128,256]{2,1,0:T(8,128)(2,1)S(1)}, bf16[4,128,256]{2,1,0:T(8,128)(2,1)S(1)}, u32[]{:S(2)}, u32[]{:S(2)}) collective-permute-start(bf16[4,128,256]{2,1,0:T(8,128)(2,1)S(1)} %get-tuple-element.1223), channel_id=1, source_target_pairs={{0,2},{1,3},{2,0},{3,1},{4,6},{5,7},{6,4},{7,5},{8,10},{9,11},{10,... | collective-permute-start | bytes 786440 | tf_op jit(solution)/shard_map/ppermute | solution.py:275
  308.1 12.2 %collective-permute-start.28 = (bf16[4,128,256]{2,1,0:T(8,128)(2,1)S(1)}, bf16[4,128,256]{2,1,0:T(8,128)(2,1)}, u32[]{:S(2)}, u32[]{:S(2)}) collective-permute-start(bf16[4,128,256]{2,1,0:T(8,128)(2,1)S(1)} %get-tuple-element.1222), channel_id=1, source_target_pairs={{0,3},{1,0},{2,1},{3,2},{4,7},{5,4},{6,5},{7,6},{8,11},{9,8},{10,9... | collective-permute-start | bytes 786440 | tf_op jit(solution)/shard_map/ppermute | solution.py:275
  308.9 14.3 %collective-permute-start.23 = (bf16[4,128,256]{2,1,0:T(8,128)(2,1)}, bf16[4,128,256]{2,1,0:T(8,128)(2,1)S(1)}, u32[]{:S(2)}, u32[]{:S(2)}) collective-permute-start(bf16[4,128,256]{2,1,0:T(8,128)(2,1)} %get-tuple-element.1228), channel_id=1, source_target_pairs={{0,1},{1,2},{2,3},{3,0},{4,5},{5,6},{6,7},{7,4},{8,9},{9,10},{10,1... | collective-permute-start | bytes 786440 | tf_op jit(solution)/shard_map/ppermute | solution.py:275
  310.4 19.0 %collective-permute-start.24 = (bf16[4,128,256]{2,1,0:T(8,128)(2,1)}, bf16[4,128,256]{2,1,0:T(8,128)(2,1)S(1)}, u32[]{:S(2)}, u32[]{:S(2)}) collective-permute-start(bf16[4,128,256]{2,1,0:T(8,128)(2,1)} %get-tuple-element.1227), channel_id=1, source_target_pairs={{0,2},{1,3},{2,0},{3,1},{4,6},{5,7},{6,4},{7,5},{8,10},{9,11},{10,... | collective-permute-start | bytes 786440 | tf_op jit(solution)/shard_map/ppermute | solution.py:275
  312.1 8.2 %copy-start.5 = (bf16[4,128,256]{2,1,0:T(8,128)(2,1)}, bf16[4,128,256]{2,1,0:T(8,128)(2,1)S(1)}, u32[]{:S(2)}) copy-start(bf16[4,128,256]{2,1,0:T(8,128)(2,1)S(1)} %collective-permute-done.26.refs_1_) | copy-start | bytes 786436
  312.1 17.3 %collective-permute-start.25 = (bf16[4,128,256]{2,1,0:T(8,128)(2,1)S(1)}, bf16[4,128,256]{2,1,0:T(8,128)(2,1)S(1)}, u32[]{:S(2)}, u32[]{:S(2)}) collective-permute-start(bf16[4,128,256]{2,1,0:T(8,128)(2,1)S(1)} %get-tuple-element.1226), channel_id=1, source_target_pairs={{0,3},{1,0},{2,1},{3,2},{4,7},{5,4},{6,5},{7,6},{8,11},{9,8},{10,9... | collective-permute-start | bytes 786440 | tf_op jit(solution)/shard_map/ppermute | solution.py:275
  323.2 6.2 %copy-start.7 = (bf16[4,128,256]{2,1,0:T(8,128)(2,1)}, bf16[4,128,256]{2,1,0:T(8,128)(2,1)S(1)}, u32[]{:S(2)}) copy-start(bf16[4,128,256]{2,1,0:T(8,128)(2,1)S(1)} %collective-permute-done.23.refs_1_) | copy-start | bytes 786436
  329.4 0.8 copy-start.9
  (2 other events, 1.4 us)
